TPU v7x, 256 devices: a whole 4x4x8 slice. The times are simulated.
256 devices in a mesh: dom: 128 (over z, y, x), ord: 2 (over core).
Axes of the slice: x: 4, y: 4, z: 8, core: 2. Of those that a mesh axis runs over, the one named last changes fastest.
Arguments:
- polar_images: bfloat16 [1024, 128, 512], P(('dom', 'ord')), may hold values from -6 to 6
- radial_basis: bfloat16 [256, 128, 128], P('ord'), may hold values from -0.5 to 0.5
- radial_start: int32 [256], P('ord'), may hold values from 0 to 4, as said below
- radial_count: int32 [256], P('ord'), may hold values from 32 to 128
- order_of_slot: int32 [256], replicated, may hold values from 0 to 255, each once
- start_block: float32 [256, 16, 128], P('ord'), may hold values from -6 to 6
Outputs:
- denoised: bfloat16 [1024, 128, 512], P(('dom', 'ord'))
Inputs may be any that keep to these rules, and one draw needn't show every extreme that they name: `radial_start`: every slot keeps at least 64 radial samples.
All inputs are finite; a program needn't handle non-finite values.
Results may differ from a plain program's by a relative error of at most 0.01.
Values may be sent and summed in bfloat16 or wider, within the bound.
A program may use at most 64 MiB of HBM per device.

v0:
```python
import math

import jax
import jax.numpy as jnp
from jax import lax
from jax.sharding import PartitionSpec as P

NRB = 8
ITERS = 4


def make_table(order_of_slot, angles):
    steps_t = jnp.arange(angles, dtype=jnp.int32)
    phase_int = steps_t[:, None] * order_of_slot[None, :] % angles
    radians = phase_int.astype(jnp.float32) * (2.0 * math.pi / angles)
    weight = math.sqrt(2.0 / angles)
    paired = jnp.stack([jnp.cos(radians) * weight, -jnp.sin(radians) * weight], axis=2)
    return paired.reshape(angles, -1).astype(jnp.bfloat16)


def masked_basis(radial_basis, radial_start, radial_count, blocks):
    radial_rows = radial_basis.shape[1]
    slot_cols = radial_basis.shape[2]
    row_ids = jnp.arange(radial_rows, dtype=jnp.int32)
    col_ids = jnp.arange(slot_cols, dtype=jnp.int32)
    keep_rows = row_ids[None, :, None] >= radial_start[:, None, None] * (radial_rows // blocks)
    keep_cols = col_ids[None, None, :] < radial_count[:, None, None]
    return jnp.where(keep_rows & keep_cols, radial_basis, jnp.zeros_like(radial_basis))


def orthonormal(image_t):
    gram_matrix = jnp.einsum("srq,stq->srt", image_t, image_t, precision=lax.Precision.HIGHEST)
    factor = jnp.linalg.cholesky(gram_matrix)
    return jax.scipy.linalg.solve_triangular(factor, image_t, lower=True)


def subspace(cov_mat, start_t):
    basis_t = start_t
    for step in range(ITERS):
        image_t = jnp.einsum("srm,smq->srq", basis_t, cov_mat, precision=lax.Precision.HIGHEST)
        basis_t = orthonormal(image_t)
    return basis_t


def radial_images(eig_t, masked):
    return jnp.einsum("stq,srq->str", eig_t, masked, preferred_element_type=jnp.float32).astype(
        jnp.bfloat16
    )


def on_device(polar_images, radial_basis, radial_start, radial_count, order_of_slot, start_block):
    particles, radial_rows, angles = polar_images.shape
    dft_table = make_table(order_of_slot, angles)
    spectrum = jnp.dot(
        polar_images.reshape(particles * radial_rows, angles),
        dft_table,
        preferred_element_type=jnp.float32,
    )
    spectrum = spectrum.astype(jnp.bfloat16).reshape(particles, radial_rows, -1)
    regrouped = lax.all_to_all(spectrum, "ord", split_axis=2, concat_axis=0, tiled=True)
    owned_slots = radial_basis.shape[0]
    group_rows = regrouped.shape[0]
    local_spec = regrouped.reshape(group_rows, radial_rows, owned_slots, 2)
    masked = masked_basis(radial_basis, radial_start, radial_count, NRB)
    coef_four = jnp.einsum(
        "prsc,srq->scpq", local_spec, masked, preferred_element_type=jnp.float32
    ).astype(jnp.bfloat16)
    coef_rows = coef_four.reshape(owned_slots, 2 * group_rows, -1)
    partial_value = jnp.einsum(
        "snq,snm->sqm", coef_rows, coef_rows, preferred_element_type=jnp.float32
    )
    cov_mine = lax.psum_scatter(partial_value, "dom", scatter_dimension=0, tiled=True)
    share_count = cov_mine.shape[0]
    first_slot = lax.axis_index("dom") * share_count
    mine_start = lax.dynamic_slice_in_dim(start_block, first_slot, share_count, 0)
    mine_basis = lax.dynamic_slice_in_dim(masked, first_slot, share_count, 0)
    eig_mine = subspace(cov_mine, mine_start).astype(jnp.bfloat16)
    u_mine = radial_images(eig_mine, mine_basis)
    eig_t, u_t = (
        lax.all_gather(eig_mine, "dom", axis=0, tiled=True),
        lax.all_gather(u_mine, "dom", axis=0, tiled=True),
    )
    scores = jnp.einsum(
        "scpq,stq->psct", coef_four, eig_t, preferred_element_type=jnp.float32
    ).astype(jnp.bfloat16)
    local_profile = jnp.einsum(
        "psct,str->prsc", scores, u_t, preferred_element_type=jnp.float32
    ).astype(jnp.bfloat16)
    local_profile = local_profile.reshape(group_rows, radial_rows, -1)
    profile = lax.all_to_all(local_profile, "ord", split_axis=0, concat_axis=2, tiled=True).reshape(
        particles * radial_rows, -1
    )
    denoised = lax.dot_general(
        profile, dft_table, (((1,), (1,)), ((), ())), preferred_element_type=jnp.float32
    )
    return denoised.astype(jnp.bfloat16).reshape(particles, radial_rows, angles)


def solution(mesh):
    placed = (
        P(("dom", "ord"), None, None),
        P("ord", None, None),
        P("ord"),
        P("ord"),
        P(),
        P("ord", None, None),
    )
    return jax.shard_map(
        on_device,
        mesh=mesh,
        in_specs=placed,
        out_specs=P(("dom", "ord"), None, None),
        check_vma=False,
    )
```

profile of v0, /device:TPU:1, one launch (start us, length us, event | category | flops | bytes accessed | tf_op | source)
XLA Modules:
  0.0 1476.3 jit_solution(6241815372960781831)
XLA Ops:
  6.5 0.0 copy-start
  6.5 0.0 copy-start.2
  6.5 3.0 multiply_convert_fusion.1
  9.6 0.1 pad_maximum_fusion
  9.7 0.5 copy.48
  10.2 0.2 convert_element_type.65
  10.4 1.5 convolution_convert_fusion.3
  11.9 1.1 copy.49
  13.0 6.7 all-to-all-start
  19.6 0.0 reduce-scatter.2.cloned.1.call-start
  19.6 0.0 copy-done.3
  19.6 1.4 all-to-all-done
  21.0 0.2 copy.50
  21.2 0.0 copy-done.2
  21.2 0.1 iota_compare_fusion
  21.3 6.0 and_select_fusion
  27.4 0.0 copy-start.1
  27.4 2.0 copy-done.1
  29.3 1.2 fusion.2
  30.5 4.5 fusion.12
  35.1 0.0 reduce-scatter.2.cloned.1.call-update
  35.1 620.3 %reduce-scatter.2.cloned.1.call-done = f32[1,128,128]{2,1,0:T(8,128)} async-done(((f32[128,128,128]{2,1,0:T(8,128)}), f32[1,128,128]{2,1,0:T(8,128)}) %reduce-scatter.2.cloned.1.call-update) | async-done | bytes 65552 | tf_op jit(solution)/shard_map/reduce_scatter | solution.py:72
  655.4 0.0 copy-done
  655.4 1.0 fusion.25
  656.4 0.1 fusion.51
  656.5 0.1 copy.52
  656.6 1.5 custom-call.12
  658.1 0.6 compare_reduce_fusion.3
  658.8 0.6 select_select_fusion.3
  659.4 1.2 custom-call.13
  660.6 0.2 fusion.38
  660.8 1.0 fusion.23
  661.8 0.1 fusion.52
  662.0 0.1 copy.54
  662.1 1.5 custom-call.14
  663.6 0.6 compare_reduce_fusion.2
  664.2 0.6 select_select_fusion.2
  664.9 1.2 custom-call.15
  666.1 0.2 fusion.36
  666.3 1.0 fusion.21
  667.3 0.1 fusion.53
  667.5 0.1 copy.56
  667.5 1.5 custom-call.16
  669.0 0.6 compare_reduce_fusion.1
  669.7 0.6 select_select_fusion.1
  670.3 1.2 custom-call.17
  671.6 0.2 fusion.34
  671.8 1.0 fusion.19
  672.8 0.1 fusion.54
  672.9 0.1 copy.58
  673.0 1.5 custom-call.18
  674.5 0.6 compare_reduce_fusion
  675.2 0.6 select_select_fusion
  675.8 1.2 custom-call.19
  677.0 0.2 fusion.6
  677.2 0.9 convolution_convert_fusion.4
  678.1 287.7 %all_gather.7 = bf16[128,16,128]{2,1,0:T(8,128)(2,1)S(1)} all-gather(bf16[1,16,128]{2,1,0:T(8,128)(2,1)S(1)} %fusion.6), channel_id=1, replica_groups=mesh['dom'=128,'ord'=2] {'dom'}, dimensions={0}, use_global_device_ids=true | all-gather | bytes 528384 | tf_op jit(solution)/shard_map/all_gather | solution.py:80
  965.9 285.6 %all-gather = bf16[2048,128]{1,0:T(8,128)(2,1)S(1)} all-gather(bf16[16,128]{1,0:T(8,128)(2,1)S(1)} %convolution_convert_fusion.4), channel_id=2, replica_groups=mesh['dom'=128,'ord'=2] {'dom'}, dimensions={0}, use_global_device_ids=true | all-gather | bytes 528384 | tf_op jit(solution)/shard_map/all_gather | solution.py:81
  1251.4 1.3 convolution_convert_fusion.1
  1252.7 1.3 copy.59
  1254.1 213.6 %all_to_all.30 = bf16[8,128,256]{2,1,0:T(8,128)(2,1)S(1)} all-to-all(bf16[8,128,256]{2,1,0:T(8,128)(2,1)S(1)} %copy.59), channel_id=1, replica_groups=mesh['dom'=128,'ord'=2] {'ord'}, dimensions={0} | all-to-all | bytes 1048576 | tf_op jit(solution)/shard_map/all_to_all | solution.py:90
  1467.6 0.5 copy.60
  1468.2 0.1 copy.68
  1468.3 1.2 convolution_convert_fusion
  (10 shorter events, 0.2 us)
Async XLA Ops:
  6.5 648.9 %copy-start = (f32[128,16,128]{2,1,0:T(8,128)S(1)}, f32[128,16,128]{2,1,0:T(8,128)}, u32[]{:S(2)}) copy-start(f32[128,16,128]{2,1,0:T(8,128)} %param.14) | copy-start | bytes 3145732
  6.5 13.1 copy-start.3
  6.5 14.7 copy-start.2
  13.0 8.1 all-to-all-start
  19.6 635.7 %reduce-scatter.2.cloned.1.call-start = ((), (), s32[]{:S(2)}) async-start(), calls=%async_computation.3 | async-start | bytes 8454144 | tf_op jit(solution)/shard_map/reduce_scatter | solution.py:72
  27.4 2.0 copy-start.1
Sparse Core Ops, SparseCore 0:
  35.2 620.1 reduce-scatter.1
where the time goes:
time: 1480 us
  blocking collectives  787 us (53%)
  waiting for transfers between devices  622 us (42%)
  other arithmetic  25.4 us (2%)
  matrix products  16.1 us (1%)
    reduce_scatter x1, waiting for transfers between devices, on_device(): lax.psum_scatter(partial_value, 'dom', scatter_dimension=0, tiled=True)  620 us
    all_gather x1, blocking collectives, on_device(): lax.all_gather(eig_mine, 'dom', axis=0, tiled=True)  288 us
    all_gather x1, blocking collectives, on_device(): lax.all_gather(u_mine, 'dom', axis=0, tiled=True)  286 us
    all_to_all x1, blocking collectives, on_device(): lax.all_to_all(local_profile, 'ord', split_axis=0, concat_axis=2, tiled=T...  214 us
  transfers between devices with their start and end apart: 2, of which 2 were waited for; matrix products, arithmetic and copies ran while one was open for 0% of the time, Pallas kernels for 0%

commit v1 on v0

v1 whole, which is shorter than its diff:
```python
import functools
import math

import jax
import jax.numpy as jnp
from jax import lax
from jax.experimental import pallas as pl
from jax.experimental.pallas import tpu as pltpu
from jax.sharding import PartitionSpec as P

NRB = 8
ITERS = 4
NZ, NY, NX = 8, 4, 4
NDOM = NZ * NY * NX
NDEV = 2 * NDOM
MESH = pl.DeviceIdType.MESH


def make_table(order_of_slot, angles):
    steps_t = jnp.arange(angles, dtype=jnp.int32)
    phase_int = order_of_slot[:, None] * steps_t[None, :] % angles
    radians = phase_int.astype(jnp.float32) * (2.0 * math.pi / angles)
    weight = math.sqrt(2.0 / angles)
    return jnp.stack([jnp.cos(radians) * weight, -jnp.sin(radians) * weight]).astype(jnp.bfloat16)


def orthonormal(image_t):
    gram_matrix = jnp.einsum("srq,stq->srt", image_t, image_t, precision=lax.Precision.HIGHEST)
    factor = jnp.linalg.cholesky(gram_matrix)
    return jax.scipy.linalg.solve_triangular(factor, image_t, lower=True)


def subspace(cov_mat, start_t):
    basis_t = start_t
    for step in range(ITERS):
        image_t = jnp.einsum("srm,smq->srq", basis_t, cov_mat, precision=lax.Precision.HIGHEST)
        basis_t = orthonormal(image_t)
    return basis_t


def exchange_kernel(src_ref, dst_ref, send_sem, recv_sem, own_sem):
    d = lax.axis_index("dom")
    o = lax.axis_index("ord")
    z, y, x = d // (NY * NX), (d // NX) % NY, d % NX
    mine = o * NDOM + d

    def peer(i):
        pz = (z + i % NZ) % NZ
        py = (y + (i // NZ) % NY) % NY
        px = (x + (i // (NZ * NY)) % NX) % NX
        po = (o + i // NDOM) % 2
        return (pz * NY + py) * NX + px, po

    barrier = pltpu.get_barrier_semaphore()

    def greet(i, carry):
        pl.semaphore_signal(barrier, inc=1, device_id=peer(i), device_id_type=MESH)
        return carry

    lax.fori_loop(1, NDEV, greet, 0)
    own = pltpu.make_async_copy(src_ref.at[mine], dst_ref.at[mine], own_sem)
    own.start()
    pl.semaphore_wait(barrier, NDEV - 1)

    def send(i, carry):
        pd, po = peer(i)
        pltpu.make_async_remote_copy(
            src_ref=src_ref.at[po * NDOM + pd],
            dst_ref=dst_ref.at[mine],
            send_sem=send_sem,
            recv_sem=recv_sem,
            device_id=(pd, po),
            device_id_type=MESH,
        ).start()
        return carry

    lax.fori_loop(1, NDEV, send, 0)
    own.wait()
    most = pl.ds(0, NDEV - 1)
    everything = pltpu.make_async_remote_copy(
        src_ref=src_ref.at[most],
        dst_ref=dst_ref.at[most],
        send_sem=send_sem,
        recv_sem=recv_sem,
        device_id=(d, 1 - o),
        device_id_type=MESH,
    )
    everything.wait_send()
    everything.wait_recv()


def exchange(blocks, collective_id):
    return pl.pallas_call(
        exchange_kernel,
        out_shape=jax.ShapeDtypeStruct(blocks.shape, blocks.dtype),
        in_specs=[pl.BlockSpec(memory_space=pltpu.VMEM)],
        out_specs=pl.BlockSpec(memory_space=pltpu.VMEM),
        scratch_shapes=[pltpu.SemaphoreType.DMA, pltpu.SemaphoreType.DMA, pltpu.SemaphoreType.DMA],
        compiler_params=pltpu.CompilerParams(collective_id=collective_id, has_side_effects=True),
        name=f"exchange_{collective_id}",
    )(blocks)


def on_device(polar_images, radial_basis, radial_start, radial_count, order_of_slot, start_block):
    particles, radial_rows, angles = polar_images.shape
    table = make_table(order_of_slot, angles)
    spectrum = jnp.einsum(
        "cst,prt->scpr", table, polar_images, preferred_element_type=jnp.float32
    ).astype(jnp.bfloat16)
    rows = exchange(spectrum.reshape(NDEV, 2 * particles, radial_rows), 0)
    rows = rows.reshape(NDEV * 2 * particles, radial_rows)

    slot = lax.axis_index("dom")
    basis = lax.dynamic_index_in_dim(radial_basis, slot, 0, keepdims=False)
    first_row = lax.dynamic_index_in_dim(radial_start, slot, 0, keepdims=False) * (radial_rows // NRB)
    count = lax.dynamic_index_in_dim(radial_count, slot, 0, keepdims=False)
    start_t = lax.dynamic_index_in_dim(start_block, slot, 0, keepdims=True)
    keep_rows = jnp.arange(radial_rows)[:, None] >= first_row
    keep_cols = jnp.arange(basis.shape[1])[None, :] < count
    masked = jnp.where(keep_rows & keep_cols, basis, jnp.zeros_like(basis))

    coef = jnp.dot(rows, masked, preferred_element_type=jnp.float32).astype(jnp.bfloat16)
    cov = jnp.einsum("nq,nm->qm", coef, coef, preferred_element_type=jnp.float32)
    eig_t = subspace(cov[None], start_t)[0].astype(jnp.bfloat16)
    u_t = jnp.einsum("tq,rq->tr", eig_t, masked, preferred_element_type=jnp.float32).astype(jnp.bfloat16)
    scores = jnp.einsum("nq,tq->nt", coef, eig_t, preferred_element_type=jnp.float32).astype(jnp.bfloat16)
    profile = jnp.dot(scores, u_t, preferred_element_type=jnp.float32).astype(jnp.bfloat16)

    mine = exchange(profile.reshape(NDEV, 2 * particles, radial_rows), 1)
    mine = mine.reshape(NDEV, 2, particles, radial_rows)
    denoised = jnp.einsum("scpr,cst->prt", mine, table, preferred_element_type=jnp.float32)
    return denoised.astype(jnp.bfloat16)


def solution(mesh):
    placed = (
        P(("dom", "ord"), None, None),
        P("ord", None, None),
        P("ord"),
        P("ord"),
        P(),
        P("ord", None, None),
    )
    return jax.shard_map(
        on_device,
        mesh=mesh,
        in_specs=placed,
        out_specs=P(("dom", "ord"), None, None),
        check_vma=False,
    )
```

time: 1480 us -> 104 us (0.07)
  blocking collectives: 787 us -> 0 us
  waiting for transfers between devices: 622 us -> 0 us
  Pallas kernels: 0 us -> 69.1 us
    reduce_scatter x1 -> x0, waiting for transfers between devices: 620 us -> none  [on_device(): lax.psum_scatter(partial_value, 'dom', scatter_dimension=0, tiled=True)]
    all_gather x2 -> x0, blocking collectives: 573 us -> none  [the longest x1 288 us: on_device(): lax.all_gather(eig_mine, 'dom', axis=0, tiled=True)]
    all_to_all x1 -> x0, blocking collectives: 214 us -> none  [on_device(): lax.all_to_all(local_profile, 'ord', split_axis=0, concat_axis=2, tiled=T...]
    pallas_call x0 -> x2, Pallas kernels: none -> 69.1 us  [exchange(): pl.pallas_call(exchange_kernel, out_shape=jax.ShapeDtypeStruct(blocks.sha...]
  transfers between devices with their start and end apart: 2 -> 0, of which waited for: 2 -> 0; matrix products, arithmetic and copies ran while one was open for 0% -> 0% of each run, Pallas kernels for 0% -> 0%
where the time goes in v1:
time: 104 us
  Pallas kernels  69.1 us (66%)
  other arithmetic  20 us (19%)
  matrix products  9.91 us (10%)
  local copies, waits for them, and re-layouts  4.14 us (4%)
    pallas_call x2, Pallas kernels, exchange(): pl.pallas_call(exchange_kernel, out_shape=jax.ShapeDtypeStruct(blocks.sha...  69.1 us
    another operation x12, other arithmetic, orthonormal(): factor = jnp.linalg.cholesky(gram_matrix)  8.58 us
    another operation x8, other arithmetic, orthonormal(): return jax.scipy.linalg.solve_triangular(factor, image_t, lower=True)  7.51 us
    another operation x1, other arithmetic  3.19 us
    dot_general x1, matrix products, on_device(): jnp.einsum('scpr,cst->prt', mine, table, preferred_element_type=jnp.float32)  2.31 us

profile of v1, /device:TPU:1, one launch (start us, length us, event | category | flops | bytes accessed | tf_op | source)
XLA Modules:
  0.0 104.0 jit_solution(17763160148559644308)
XLA Ops:
  0.0 0.0 copy-start
  0.0 1.3 %dynamic_slice.16 = s32[1]{0:T(128)} dynamic-slice(s32[128]{0:T(128)} %param.12, s32[]{:T(128)S(6)} %select_n.39), dynamic_slice_sizes={1} | dynamic-slice | bytes 12 | tf_op jit(solution)/shard_map/jit(dynamic_index_in_dim)/dynamic_slice | solution.py:116
  1.3 1.3 %dynamic_slice.15 = s32[1]{0:T(128)} dynamic-slice(s32[128]{0:T(128)} %param.11, s32[]{:T(128)S(6)} %select_n.39), dynamic_slice_sizes={1} | dynamic-slice | bytes 12 | tf_op jit(solution)/shard_map/jit(dynamic_index_in_dim)/dynamic_slice | solution.py:115
  3.3 0.7 iota_compare_fusion.2
  4.0 3.2 %multiply_convert_fusion.1 = (bf16[1,256,512]{2,1,0:T(8,128)(2,1)S(1)}, bf16[1,256,512]{2,1,0:T(8,128)(2,1)S(1)}) fusion(s32[256]{0:T(256)} %param.13), kind=kLoop, calls=%fused_computation.25 | loop fusion | flops 2490368 | bytes 525312 | tf_op jit(solution)/shard_map/convert
  7.2 1.5 %fusion.2 = bf16[256,2,4,128]{3,0,2,1:T(8,128)(2,1)S(1)} fusion(bf16[4,128,512]{2,1,0:T(8,128)(2,1)} %param.9, bf16[1,256,512]{2,1,0:T(8,128)(2,1)S(1)} %get-tuple-element.8, bf16[1,256,512]{2,1,0:T(8,128)(2,1)S(1)} %get-tuple-element.6), kind=kOutput, calls=%fused_computation.7 | convolution fusion | flops 269746176 | bytes 1572864 | tf_op jit(solution)/shard_map/cst,prt->scpr/dot_general | solution.py:107
  8.7 1.2 %copy.7 = bf16[256,2,4,128]{3,2,1,0:T(4,128)(2,1)} copy(bf16[256,2,4,128]{3,0,2,1:T(8,128)(2,1)S(1)} %fusion.2) | data formatting | bytes 1048576 | tf_op jit(solution)/shard_map/convert_element_type | solution.py:109
  9.9 37.6 %exchange_0.1 = bf16[256,8,128]{2,1,0:T(8,128)(2,1)} custom-call(bf16[256,8,128]{2,1,0:T(8,128)(2,1)} %bitcast.109), custom_call_target="tpu_custom_call" | custom-call | tf_op jit(solution)/shard_map/exchange_0/pallas_call | solution.py:93
  47.6 1.4 %convolution_convert_fusion.2 = bf16[2048,128]{1,0:T(8,128)(2,1)S(1)} fusion(bf16[256,8,128]{2,1,0:T(8,128)(2,1)} %exchange_0.1, bf16[128,128,128]{2,1,0:T(8,128)(2,1)} %param.10, s32[]{:T(128)S(6)} %select_n.39, pred[128]{0:T(512)(128)(4,1)S(1)} %get-tuple-element.9, pred[128]{0:T(512)(128)(4,1)S(1)} %get-tuple-element.10), kind=kOutput, calls=%fused_computation.2 | convolution fusion | flops 67403776 | bytes 1081604 | tf_op jit(solution)/shard_map/dot_general | solution.py:122
  49.0 0.3 fusion.46
  49.3 0.0 copy-done
  49.3 0.2 fusion.28
  49.5 0.1 fusion.47
  49.6 0.1 copy.9
  49.7 1.5 %custom-call.12 = f32[1,16,16]{2,1,0:T(8,128)S(1)} custom-call(f32[1,16,16]{2,1,0:T(8,128)S(1)} %fusion.20), custom_call_target="Cholesky" | custom-call | tf_op jit(solution)/shard_map/jit(cholesky)/cholesky | solution.py:29
  51.2 0.6 compare_reduce_fusion.3
  51.9 0.6 select_select_fusion.3
  52.5 1.2 %custom-call.13 = f32[1,16,16]{1,2,0:T(8,128)S(1)} custom-call(f32[1,16,16]{2,1,0:T(8,128)S(1)} %select_select_fusion.3), custom_call_target="InvertDiagBlocksLowerTriangular" | custom-call | tf_op jit(solution)/shard_map/jit(_solve_triangular)/triangular_solve | solution.py:30
  53.7 0.2 fusion.26
  53.9 0.2 fusion.48
  54.1 0.1 fusion.49
  54.3 0.1 copy.11
  54.3 1.5 %custom-call.14 = f32[1,16,16]{2,1,0:T(8,128)S(1)} custom-call(f32[1,16,16]{2,1,0:T(8,128)S(1)} %fusion.19), custom_call_target="Cholesky" | custom-call | tf_op jit(solution)/shard_map/jit(cholesky)/cholesky | solution.py:29
  55.8 0.6 compare_reduce_fusion.2
  56.5 0.6 select_select_fusion.2
  57.1 1.2 %custom-call.15 = f32[1,16,16]{1,2,0:T(8,128)S(1)} custom-call(f32[1,16,16]{2,1,0:T(8,128)S(1)} %select_select_fusion.2), custom_call_target="InvertDiagBlocksLowerTriangular" | custom-call | tf_op jit(solution)/shard_map/jit(_solve_triangular)/triangular_solve | solution.py:30
  58.4 0.2 fusion.24
  58.6 0.2 fusion.50
  58.7 0.1 fusion.51
  58.9 0.1 copy.13
  59.0 1.5 %custom-call.16 = f32[1,16,16]{2,1,0:T(8,128)S(1)} custom-call(f32[1,16,16]{2,1,0:T(8,128)S(1)} %fusion.18), custom_call_target="Cholesky" | custom-call | tf_op jit(solution)/shard_map/jit(cholesky)/cholesky | solution.py:29
  60.5 0.6 compare_reduce_fusion.1
  61.1 0.6 select_select_fusion.1
  61.8 1.2 %custom-call.17 = f32[1,16,16]{1,2,0:T(8,128)S(1)} custom-call(f32[1,16,16]{2,1,0:T(8,128)S(1)} %select_select_fusion.1), custom_call_target="InvertDiagBlocksLowerTriangular" | custom-call | tf_op jit(solution)/shard_map/jit(_solve_triangular)/triangular_solve | solution.py:30
  63.0 0.2 fusion.22
  63.2 0.2 fusion.52
  63.4 0.1 fusion.53
  63.5 0.1 copy.15
  63.6 1.5 %custom-call.18 = f32[1,16,16]{2,1,0:T(8,128)S(1)} custom-call(f32[1,16,16]{2,1,0:T(8,128)S(1)} %fusion.17), custom_call_target="Cholesky" | custom-call | tf_op jit(solution)/shard_map/jit(cholesky)/cholesky | solution.py:29
  65.1 0.6 compare_reduce_fusion
  65.8 0.6 select_select_fusion
  66.4 1.2 %custom-call.19 = f32[1,16,16]{1,2,0:T(8,128)S(1)} custom-call(f32[1,16,16]{2,1,0:T(8,128)S(1)} %select_select_fusion), custom_call_target="InvertDiagBlocksLowerTriangular" | custom-call | tf_op jit(solution)/shard_map/jit(_solve_triangular)/triangular_solve | solution.py:30
  67.6 0.2 fusion.4
  67.8 1.0 convolution_convert_fusion.4
  68.8 1.3 %fusion.1.src_ref = bf16[256,8,128]{2,1,0:T(8,128)(2,1)} fusion(bf16[16,128]{1,0:T(8,128)(2,1)S(1)} %convolution_convert_fusion.4, bf16[2048,128]{1,0:T(8,128)(2,1)S(1)} %convolution_convert_fusion.2, bf16[16,128]{1,0:T(8,128)(2,1)S(1)} %fusion.4), kind=kOutput, calls=%fused_computation.6 | convolution fusion | flops 17072128 | bytes 1056768 | tf_op jit(solution)/shard_map/dot_general | solution.py:127
  70.1 31.5 %exchange_1.1 = bf16[256,8,128]{2,1,0:T(8,128)(2,1)} custom-call(bf16[256,8,128]{2,1,0:T(8,128)(2,1)} %fusion.1.src_ref), custom_call_target="tpu_custom_call" | custom-call | tf_op jit(solution)/shard_map/exchange_1/pallas_call | solution.py:93
  101.6 2.3 %fusion = bf16[4,128,512]{2,1,0:T(8,128)(2,1)} fusion(bf16[256,2,4,128]{3,2,1,0:T(4,128)(2,1)} %bitcast.110, bf16[1,256,512]{2,1,0:T(8,128)(2,1)S(1)} %get-tuple-element.8, bf16[1,256,512]{2,1,0:T(8,128)(2,1)S(1)} %get-tuple-element.6), kind=kOutput, calls=%fused_computation.5 | convolution fusion | flops 268959744 | bytes 1572864 | tf_op jit(solution)/shard_map/scpr,cst->prt/dot_general | solution.py:131
  (8 shorter events, 0.2 us)
Async XLA Ops:
  0.0 49.3 %copy-start = (f32[128,16,128]{2,1,0:T(8,128)S(1)}, f32[128,16,128]{2,1,0:T(8,128)}, u32[]{:S(2)}) copy-start(f32[128,16,128]{2,1,0:T(8,128)} %param.14) | copy-start | bytes 3145732

commit v2 on v1

v2 whole, which is shorter than its diff:
```python
import math

import jax
import jax.numpy as jnp
from jax import lax
from jax.experimental import pallas as pl
from jax.experimental.pallas import tpu as pltpu
from jax.sharding import PartitionSpec as P

NRB = 8
ITERS = 4
NZ, NY, NX = 8, 4, 4
NDOM = NZ * NY * NX
NDEV = 2 * NDOM
MESH = pl.DeviceIdType.MESH


def make_table(order_of_slot, angles):
    steps_t = jnp.arange(angles, dtype=jnp.int32)
    phase_int = order_of_slot[:, None] * steps_t[None, :] % angles
    radians = phase_int.astype(jnp.float32) * (2.0 * math.pi / angles)
    weight = math.sqrt(2.0 / angles)
    return jnp.stack([jnp.cos(radians) * weight, -jnp.sin(radians) * weight]).astype(jnp.bfloat16)


FAR_FIRST_8 = (4, 3, 5, 2, 6, 1, 7, 0)
FAR_FIRST_4 = (2, 1, 3, 0)


def dot32(a, b, dims):
    return lax.dot_general(
        a, b, (dims, ((), ())), precision=lax.Precision.HIGHEST, preferred_element_type=jnp.float32
    )


def orthonormal(image_t):
    rank, width = image_t.shape
    gram = dot32(image_t, image_t, ((1,), (1,)))
    lane_block = lax.broadcasted_iota(jnp.int32, (rank, rank * width), 1) // width
    spread = lane_block == lax.broadcasted_iota(jnp.int32, (rank, rank * width), 0)
    wide = dot32(gram, spread.astype(jnp.float32), ((1,), (0,)))
    cols = [wide[:, j * width : (j + 1) * width] for j in range(rank)]
    row_id = lax.broadcasted_iota(jnp.int32, (rank, width), 0)
    pivots = jnp.ones((rank, width), jnp.float32)
    out = image_t
    for j in range(rank):
        pivot = jnp.broadcast_to(cols[j][j : j + 1, :], (rank, width))
        pivots = jnp.where(row_id == j, pivot, pivots)
        factor = jnp.where(row_id > j, cols[j] / pivot, 0.0)
        for k in range(j + 1, rank):
            cols[k] = cols[k] - factor * cols[k][j : j + 1, :]
        out = out - factor * out[j : j + 1, :]
    return out / jnp.sqrt(pivots)


def peers():
    d = lax.axis_index("dom")
    o = lax.axis_index("ord")
    z, y, x = d // (NY * NX), (d // NX) % NY, d % NX
    at_z = [(z + k) % NZ * (NY * NX) for k in range(NZ)]
    at_y = [(y + k) % NY * NX for k in range(NY)]
    at_x = [(x + k) % NX for k in range(NX)]
    for dy in FAR_FIRST_4:
        for dx in FAR_FIRST_4:
            plane = at_y[dy] + at_x[dx]
            for dz in FAR_FIRST_8:
                for other in (True, False):
                    if other or (dz, dy, dx) != (0, 0, 0):
                        yield at_z[dz] + plane, (1 - o if other else o)


def greet_all():
    barrier = pltpu.get_barrier_semaphore()
    for pd, po in peers():
        pl.semaphore_signal(barrier, inc=1, device_id=(pd, po), device_id_type=MESH)


def exchange_blocks(src_ref, dst_ref, send_sem, recv_sem, own_sem):
    d = lax.axis_index("dom")
    o = lax.axis_index("ord")
    mine = o * NDOM + d
    own = pltpu.make_async_copy(src_ref.at[mine], dst_ref.at[mine], own_sem)
    own.start()
    pl.semaphore_wait(pltpu.get_barrier_semaphore(), NDEV - 1)
    for pd, po in peers():
        pltpu.make_async_remote_copy(
            src_ref=src_ref.at[po * NDOM + pd],
            dst_ref=dst_ref.at[mine],
            send_sem=send_sem,
            recv_sem=recv_sem,
            device_id=(pd, po),
            device_id_type=MESH,
        ).start()
    own.wait()
    most = pl.ds(0, NDEV - 1)
    everything = pltpu.make_async_remote_copy(
        src_ref=src_ref.at[most],
        dst_ref=dst_ref.at[most],
        send_sem=send_sem,
        recv_sem=recv_sem,
        device_id=(d, 1 - o),
        device_id_type=MESH,
    )
    everything.wait_send()
    everything.wait_recv()


def exchange_kernel(src_ref, dst_ref, send_sem, recv_sem, own_sem):
    greet_all()
    exchange_blocks(src_ref, dst_ref, send_sem, recv_sem, own_sem)


def profile_kernel(
    cov_ref, start_ref, masked_ref, coef_ref, dst_ref, prof_ref, send_sem, recv_sem, own_sem
):
    greet_all()
    cov = cov_ref[...]
    basis_t = start_ref[...]
    for step in range(ITERS):
        basis_t = orthonormal(dot32(basis_t, cov, ((1,), (0,))))
    eig_t = basis_t.astype(jnp.bfloat16)
    u_t = lax.dot_general(
        eig_t, masked_ref[...], (((1,), (1,)), ((), ())), preferred_element_type=jnp.float32
    ).astype(jnp.bfloat16)
    chunk = 512
    for lo in range(0, coef_ref.shape[0], chunk):
        scores = lax.dot_general(
            coef_ref[lo : lo + chunk, :],
            eig_t,
            (((1,), (1,)), ((), ())),
            preferred_element_type=jnp.float32,
        ).astype(jnp.bfloat16)
        profile = jnp.dot(scores, u_t, preferred_element_type=jnp.float32)
        blocks = profile.reshape(chunk // 8, 8, profile.shape[1]).astype(jnp.bfloat16)
        prof_ref[lo // 8 : (lo + chunk) // 8] = blocks
    exchange_blocks(prof_ref, dst_ref, send_sem, recv_sem, own_sem)


def comm_call(kernel, collective_id, shape, *operands, scratch=(), name):
    vmem = pl.BlockSpec(memory_space=pltpu.VMEM)
    return pl.pallas_call(
        kernel,
        out_shape=jax.ShapeDtypeStruct(shape, jnp.bfloat16),
        in_specs=[vmem] * len(operands),
        out_specs=vmem,
        scratch_shapes=[*scratch, *[pltpu.SemaphoreType.DMA] * 3],
        compiler_params=pltpu.CompilerParams(collective_id=collective_id, has_side_effects=True),
        name=name,
    )(*operands)


def on_device(polar_images, radial_basis, radial_start, radial_count, order_of_slot, start_block):
    particles, radial_rows, angles = polar_images.shape
    table = make_table(order_of_slot, angles)
    spectrum = jnp.einsum(
        "cst,prt->scpr", table, polar_images, preferred_element_type=jnp.float32
    ).astype(jnp.bfloat16)
    shape = (NDEV, 2 * particles, radial_rows)
    rows = comm_call(exchange_kernel, 0, shape, spectrum.reshape(shape), name="spectra")
    rows = rows.reshape(NDEV * 2 * particles, radial_rows)

    slot = lax.axis_index("dom")
    basis = lax.dynamic_index_in_dim(radial_basis, slot, 0, keepdims=False)
    first_row = lax.dynamic_index_in_dim(radial_start, slot, 0, keepdims=False) * (radial_rows // NRB)
    count = lax.dynamic_index_in_dim(radial_count, slot, 0, keepdims=False)
    start_t = lax.dynamic_index_in_dim(start_block, slot, 0, keepdims=False)
    keep_rows = jnp.arange(radial_rows)[:, None] >= first_row
    keep_cols = jnp.arange(basis.shape[1])[None, :] < count
    masked = jnp.where(keep_rows & keep_cols, basis, jnp.zeros_like(basis))

    coef = jnp.dot(rows, masked, preferred_element_type=jnp.float32).astype(jnp.bfloat16)
    cov = jnp.einsum("nq,nm->qm", coef, coef, preferred_element_type=jnp.float32)
    mine = comm_call(
        profile_kernel,
        1,
        shape,
        cov,
        start_t,
        masked,
        coef,
        scratch=[pltpu.VMEM(shape, jnp.bfloat16)],
        name="profiles",
    )
    mine = mine.reshape(NDEV, 2, particles, radial_rows)
    denoised = jnp.einsum("scpr,cst->prt", mine, table, preferred_element_type=jnp.float32)
    return denoised.astype(jnp.bfloat16)


def solution(mesh):
    placed = (
        P(("dom", "ord"), None, None),
        P("ord", None, None),
        P("ord"),
        P("ord"),
        P(),
        P("ord", None, None),
    )
    return jax.shard_map(
        on_device,
        mesh=mesh,
        in_specs=placed,
        out_specs=P(("dom", "ord"), None, None),
        check_vma=False,
    )
```

time: 104 us -> 68.5 us (0.66)
  Pallas kernels: 69.1 us -> 51.6 us
  other arithmetic: 20 us -> 5.28 us
  matrix products: 9.91 us -> 6.18 us
    pallas_call x2, Pallas kernels: 69.1 us -> 51.6 us  [comm_call(): pl.pallas_call(kernel, out_shape=jax.ShapeDtypeStruct(shape, jnp.bfloat16...]
    another operation x21 -> x1, other arithmetic: 19.3 us -> 3.18 us  [the longest x12 8.58 us: orthonormal(): factor = jnp.linalg.cholesky(gram_matrix)]
    dot_general x10 -> x0, matrix products: 3.54 us -> none  [the longest x1 1.33 us: on_device(): jnp.dot(scores, u_t, preferred_element_type=jnp.float32)]
    select_n x0 -> x1, other arithmetic: none -> 1.44 us  [on_device(): masked = jnp.where(keep_rows & keep_cols, basis, jnp.zeros_like(basis))]
where the time goes in v2:
time: 68.5 us; the launch traced here: 68.1 us
  Pallas kernels  51.6 us (75%)
  matrix products  6.18 us (9%)
  other arithmetic  5.28 us (8%)
  local copies, waits for them, and re-layouts  4.4 us (6%)
    pallas_call x2, Pallas kernels, comm_call(): pl.pallas_call(kernel, out_shape=jax.ShapeDtypeStruct(shape, jnp.bfloat16...  51.6 us
    another operation x1, other arithmetic  3.18 us
    dot_general x1, matrix products, on_device(): jnp.einsum('scpr,cst->prt', mine, table, preferred_element_type=jnp.float32)  2.31 us
    dot_general x1, matrix products, on_device(): jnp.einsum('cst,prt->scpr', table, polar_images, preferred_element_type=j...  1.51 us
    select_n x1, other arithmetic, on_device(): masked = jnp.where(keep_rows & keep_cols, basis, jnp.zeros_like(basis))  1.44 us
    dot_general x1, matrix products, on_device(): jnp.dot(rows, masked, preferred_element_type=jnp.float32)  1.4 us

profile of v2, /device:TPU:1, one launch (start us, length us, event | category | flops | bytes accessed | tf_op | source)
XLA Modules:
  0.0 68.1 jit_solution(14774423677271365673)
XLA Ops:
  0.0 0.0 copy-start
  0.0 1.3 %dynamic_slice.16 = s32[1]{0:T(128)} dynamic-slice(s32[128]{0:T(128)} %param.9, s32[]{:T(128)S(6)} %select_n.36), dynamic_slice_sizes={1} | dynamic-slice | bytes 12 | tf_op jit(solution)/shard_map/jit(dynamic_index_in_dim)/dynamic_slice | solution.py:165
  1.3 1.3 %dynamic_slice.15 = s32[1]{0:T(128)} dynamic-slice(s32[128]{0:T(128)} %param.8, s32[]{:T(128)S(6)} %select_n.36), dynamic_slice_sizes={1} | dynamic-slice | bytes 12 | tf_op jit(solution)/shard_map/jit(dynamic_index_in_dim)/dynamic_slice | solution.py:164
  3.2 0.7 iota_compare_fusion
  3.9 0.0 copy-done
  3.9 0.6 dynamic-slice_bitcast_fusion.start_ref
  4.5 1.4 %and_select_fusion.masked_ref = bf16[128,128]{1,0:T(8,128)(2,1)} fusion(pred[128]{0:T(512)(128)(4,1)S(1)} %get-tuple-element.7, pred[128]{0:T(512)(128)(4,1)S(1)} %get-tuple-element.8, bf16[128,128,128]{2,1,0:T(8,128)(2,1)} %param.7, s32[]{:T(128)S(6)} %select_n.36), kind=kLoop, calls=%fused_computation.22 | loop fusion | flops 32768 | bytes 65796 | tf_op jit(solution)/shard_map/jit(_where)/select_n | solution.py:169
  5.9 3.2 %multiply_convert_fusion.1 = (bf16[1,256,512]{2,1,0:T(8,128)(2,1)S(1)}, bf16[1,256,512]{2,1,0:T(8,128)(2,1)S(1)}) fusion(s32[256]{0:T(256)} %param.10), kind=kLoop, calls=%fused_computation.18 | loop fusion | flops 2490368 | bytes 525312 | tf_op jit(solution)/shard_map/convert
  9.1 1.5 %fusion.1 = bf16[256,2,4,128]{3,0,2,1:T(8,128)(2,1)S(1)} fusion(bf16[4,128,512]{2,1,0:T(8,128)(2,1)} %param.6, bf16[1,256,512]{2,1,0:T(8,128)(2,1)S(1)} %get-tuple-element.6, bf16[1,256,512]{2,1,0:T(8,128)(2,1)S(1)} %get-tuple-element.5), kind=kOutput, calls=%fused_computation.4 | convolution fusion | flops 269746176 | bytes 1572864 | tf_op jit(solution)/shard_map/cst,prt->scpr/dot_general | solution.py:155
  10.6 1.2 %copy.7 = bf16[256,2,4,128]{3,2,1,0:T(4,128)(2,1)} copy(bf16[256,2,4,128]{3,0,2,1:T(8,128)(2,1)S(1)} %fusion.1) | data formatting | bytes 1048576 | tf_op jit(solution)/shard_map/convert_element_type | solution.py:157
  11.8 28.8 %spectra.1 = bf16[256,8,128]{2,1,0:T(8,128)(2,1)} custom-call(bf16[256,8,128]{2,1,0:T(8,128)(2,1)} %bitcast.33), custom_call_target="tpu_custom_call" | custom-call | tf_op jit(solution)/shard_map/spectra/pallas_call | solution.py:141
  40.6 1.4 %convolution_convert_fusion.coef_ref = bf16[2048,128]{1,0:T(8,128)(2,1)S(1)} fusion(bf16[256,8,128]{2,1,0:T(8,128)(2,1)} %spectra.1, pred[128]{0:T(512)(128)(4,1)S(1)} %get-tuple-element.7, pred[128]{0:T(512)(128)(4,1)S(1)} %get-tuple-element.8, bf16[128,128,128]{2,1,0:T(8,128)(2,1)} %param.7, s32[]{:T(128)S(6)} %select_n.36), kind=kOutput, calls=%fused_computation | convolution fusion | flops 67403776 | bytes 1081604 | tf_op jit(solution)/shard_map/dot_general | solution.py:171
  42.0 0.0 copy-start.1
  42.0 1.0 %fusion.23.cov_ref = f32[128,128]{1,0:T(8,128)} fusion(bf16[2048,128]{1,0:T(8,128)(2,1)S(1)} %convolution_convert_fusion.coef_ref), kind=kOutput, calls=%fused_computation.36 | convolution fusion | flops 67108864 | bytes 589824 | tf_op jit(solution)/shard_map/nq,nm->qm/dot_general | solution.py:172
  43.0 0.0 copy-done.1
  43.0 22.8 %profiles.1 = bf16[256,8,128]{2,1,0:T(8,128)(2,1)} custom-call(f32[128,128]{1,0:T(8,128)} %fusion.23.cov_ref, f32[16,128]{1,0:T(8,128)} %dynamic-slice_bitcast_fusion.start_ref, bf16[128,128]{1,0:T(8,128)(2,1)} %and_select_fusion.masked_ref, bf16[2048,128]{1,0:T(8,128)(2,1)} %copy-done.1), custom_call_target="tpu_custom_call" | custom-call | tf_op jit(solution)/shard_map/profiles/pallas_call | solution.py:141
  65.8 2.3 %fusion = bf16[4,128,512]{2,1,0:T(8,128)(2,1)} fusion(bf16[256,2,4,128]{3,2,1,0:T(4,128)(2,1)} %bitcast.34, bf16[1,256,512]{2,1,0:T(8,128)(2,1)S(1)} %get-tuple-element.6, bf16[1,256,512]{2,1,0:T(8,128)(2,1)S(1)} %get-tuple-element.5), kind=kOutput, calls=%fused_computation.3 | convolution fusion | flops 268959744 | bytes 1572864 | tf_op jit(solution)/shard_map/scpr,cst->prt/dot_general | solution.py:185
Async XLA Ops:
  0.0 3.9 %copy-start = (f32[128,16,128]{2,1,0:T(8,128)S(1)}, f32[128,16,128]{2,1,0:T(8,128)}, u32[]{:S(2)}) copy-start(f32[128,16,128]{2,1,0:T(8,128)} %param.11) | copy-start | bytes 3145732
  42.0 1.0 %copy-start.1 = (bf16[2048,128]{1,0:T(8,128)(2,1)}, bf16[2048,128]{1,0:T(8,128)(2,1)S(1)}, u32[]{:S(2)}) copy-start(bf16[2048,128]{1,0:T(8,128)(2,1)S(1)} %convolution_convert_fusion.coef_ref) | copy-start | bytes 1572868

commit v3 on v2

--- a/solution.py
+++ b/solution.py
@@ -13,14 +13,6 @@
 NDOM = NZ * NY * NX
 NDEV = 2 * NDOM
 MESH = pl.DeviceIdType.MESH
-
-
-def make_table(order_of_slot, angles):
-    steps_t = jnp.arange(angles, dtype=jnp.int32)
-    phase_int = order_of_slot[:, None] * steps_t[None, :] % angles
-    radians = phase_int.astype(jnp.float32) * (2.0 * math.pi / angles)
-    weight = math.sqrt(2.0 / angles)
-    return jnp.stack([jnp.cos(radians) * weight, -jnp.sin(radians) * weight]).astype(jnp.bfloat16)
 
 
 FAR_FIRST_8 = (4, 3, 5, 2, 6, 1, 7, 0)
@@ -81,7 +73,6 @@
     mine = o * NDOM + d
     own = pltpu.make_async_copy(src_ref.at[mine], dst_ref.at[mine], own_sem)
     own.start()
-    pl.semaphore_wait(pltpu.get_barrier_semaphore(), NDEV - 1)
     for pd, po in peers():
         pltpu.make_async_remote_copy(
             src_ref=src_ref.at[po * NDOM + pd],
@@ -105,24 +96,106 @@
     everything.wait_recv()
 
 
-def exchange_kernel(src_ref, dst_ref, send_sem, recv_sem, own_sem):
+def fill_table(order_ref, table_ref):
+    angles = table_ref.shape[1]
+    weight = math.sqrt(2.0 / angles)
+    for half in range(2):
+        row = order_ref[half : half + 1, :].astype(jnp.float32)
+        k = jnp.broadcast_to(row, (128, 128)).T.astype(jnp.int32)
+        lane = lax.broadcasted_iota(jnp.int32, (128, 128), 1)
+        turn = (k * lane) & (angles - 1)
+        quarter = (turn + angles // 8) >> 7
+        angle = (turn - quarter * (angles // 4)).astype(jnp.float32) * (2.0 * math.pi / angles)
+        sq = angle * angle
+        cos = 1.0 + sq * (-1 / 2 + sq * (1 / 24 + sq * (-1 / 720 + sq * (1 / 40320))))
+        sin = angle * (1.0 + sq * (-1 / 6 + sq * (1 / 120 + sq * (-1 / 5040 + sq * (1 / 362880)))))
+        cos = cos * weight
+        sin = sin * weight
+        for b in range(angles // 128):
+            quadrant = (quarter + b * k) & 3
+            odd = (quadrant & 1) == 1
+            upper = quadrant >= 2
+            even_sign = jnp.where(upper, -1.0, 1.0)
+            real = jnp.where(odd, -sin, cos) * even_sign
+            imag = jnp.where(odd, -cos, -sin) * even_sign
+            span = slice(128 * b, 128 * (b + 1))
+            table_ref[128 * half : 128 * (half + 1), span] = real.astype(jnp.bfloat16)
+            table_ref[256 + 128 * half : 256 + 128 * (half + 1), span] = imag.astype(jnp.bfloat16)
+
+
+def fill_spectrum(table_ref, images_ref, wide_ref, spec_ref):
+    for p in range(images_ref.shape[0]):
+        for c in range(2):
+            part = lax.dot_general(
+                table_ref[256 * c : 256 * (c + 1), :],
+                images_ref[p],
+                (((1,), (1,)), ((), ())),
+                preferred_element_type=jnp.float32,
+            )
+            wide_ref[pl.ds(4 * c + p, NDEV, stride=8), :] = part
+    spec_ref[...] = wide_ref[...].reshape(spec_ref.shape).astype(jnp.bfloat16)
+
+
+def whole_kernel(
+    images_ref,
+    radial_ref,
+    first_ref,
+    count_ref,
+    order_ref,
+    start_ref,
+    table_ref,
+    out_ref,
+    wide_ref,
+    spec_ref,
+    rows_ref,
+    coef_ref,
+    prof_ref,
+    radial_own,
+    start_own,
+    send_1,
+    recv_1,
+    own_1,
+    send_2,
+    recv_2,
+    own_2,
+    load_1,
+    load_2,
+):
+    slot = lax.axis_index("dom")
     greet_all()
-    exchange_blocks(src_ref, dst_ref, send_sem, recv_sem, own_sem)
-
-
-def profile_kernel(
-    cov_ref, start_ref, masked_ref, coef_ref, dst_ref, prof_ref, send_sem, recv_sem, own_sem
-):
-    greet_all()
-    cov = cov_ref[...]
-    basis_t = start_ref[...]
+    radial_load = pltpu.make_async_copy(radial_ref.at[slot], radial_own, load_1)
+    start_load = pltpu.make_async_copy(start_ref.at[slot], start_own, load_2)
+    radial_load.start()
+    start_load.start()
+    fill_table(order_ref, table_ref)
+    fill_spectrum(table_ref, images_ref, wide_ref, spec_ref)
+    radial_load.wait()
+    start_load.wait()
+    first_row = first_ref[slot] * (radial_own.shape[0] // NRB)
+    row_id = lax.broadcasted_iota(jnp.int32, radial_own.shape, 0)
+    col_id = lax.broadcasted_iota(jnp.int32, radial_own.shape, 1)
+    keep = (row_id >= first_row) & (col_id < count_ref[slot])
+    masked = jnp.where(keep, radial_own[...].astype(jnp.float32), 0.0).astype(jnp.bfloat16)
+    pl.semaphore_wait(pltpu.get_barrier_semaphore(), NDEV - 1)
+    exchange_blocks(spec_ref, rows_ref, send_1, recv_1, own_1)
+
+    chunk = 512
+    cov = jnp.zeros((masked.shape[1], masked.shape[1]), jnp.float32)
+    for lo in range(0, coef_ref.shape[0], chunk):
+        block = rows_ref[lo // 8 : (lo + chunk) // 8].astype(jnp.float32)
+        rows = block.reshape(chunk, block.shape[2]).astype(jnp.bfloat16)
+        coef = jnp.dot(rows, masked, preferred_element_type=jnp.float32).astype(jnp.bfloat16)
+        coef_ref[lo : lo + chunk, :] = coef
+        cov = cov + lax.dot_general(
+            coef, coef, (((0,), (0,)), ((), ())), preferred_element_type=jnp.float32
+        )
+    basis_t = start_own[...]
     for step in range(ITERS):
         basis_t = orthonormal(dot32(basis_t, cov, ((1,), (0,))))
     eig_t = basis_t.astype(jnp.bfloat16)
     u_t = lax.dot_general(
-        eig_t, masked_ref[...], (((1,), (1,)), ((), ())), preferred_element_type=jnp.float32
+        eig_t, masked, (((1,), (1,)), ((), ())), preferred_element_type=jnp.float32
     ).astype(jnp.bfloat16)
-    chunk = 512
     for lo in range(0, coef_ref.shape[0], chunk):
         scores = lax.dot_general(
             coef_ref[lo : lo + chunk, :],
@@ -133,55 +206,48 @@
         profile = jnp.dot(scores, u_t, preferred_element_type=jnp.float32)
         blocks = profile.reshape(chunk // 8, 8, profile.shape[1]).astype(jnp.bfloat16)
         prof_ref[lo // 8 : (lo + chunk) // 8] = blocks
-    exchange_blocks(prof_ref, dst_ref, send_sem, recv_sem, own_sem)
-
-
-def comm_call(kernel, collective_id, shape, *operands, scratch=(), name):
-    vmem = pl.BlockSpec(memory_space=pltpu.VMEM)
-    return pl.pallas_call(
-        kernel,
-        out_shape=jax.ShapeDtypeStruct(shape, jnp.bfloat16),
-        in_specs=[vmem] * len(operands),
-        out_specs=vmem,
-        scratch_shapes=[*scratch, *[pltpu.SemaphoreType.DMA] * 3],
-        compiler_params=pltpu.CompilerParams(collective_id=collective_id, has_side_effects=True),
-        name=name,
-    )(*operands)
+    exchange_blocks(prof_ref, out_ref, send_2, recv_2, own_2)
 
 
 def on_device(polar_images, radial_basis, radial_start, radial_count, order_of_slot, start_block):
     particles, radial_rows, angles = polar_images.shape
-    table = make_table(order_of_slot, angles)
-    spectrum = jnp.einsum(
-        "cst,prt->scpr", table, polar_images, preferred_element_type=jnp.float32
-    ).astype(jnp.bfloat16)
+    rank, width = start_block.shape[1:]
+    slots = order_of_slot.shape[0]
     shape = (NDEV, 2 * particles, radial_rows)
-    rows = comm_call(exchange_kernel, 0, shape, spectrum.reshape(shape), name="spectra")
-    rows = rows.reshape(NDEV * 2 * particles, radial_rows)
-
-    slot = lax.axis_index("dom")
-    basis = lax.dynamic_index_in_dim(radial_basis, slot, 0, keepdims=False)
-    first_row = lax.dynamic_index_in_dim(radial_start, slot, 0, keepdims=False) * (radial_rows // NRB)
-    count = lax.dynamic_index_in_dim(radial_count, slot, 0, keepdims=False)
-    start_t = lax.dynamic_index_in_dim(start_block, slot, 0, keepdims=False)
-    keep_rows = jnp.arange(radial_rows)[:, None] >= first_row
-    keep_cols = jnp.arange(basis.shape[1])[None, :] < count
-    masked = jnp.where(keep_rows & keep_cols, basis, jnp.zeros_like(basis))
-
-    coef = jnp.dot(rows, masked, preferred_element_type=jnp.float32).astype(jnp.bfloat16)
-    cov = jnp.einsum("nq,nm->qm", coef, coef, preferred_element_type=jnp.float32)
-    mine = comm_call(
-        profile_kernel,
-        1,
-        shape,
-        cov,
-        start_t,
-        masked,
-        coef,
-        scratch=[pltpu.VMEM(shape, jnp.bfloat16)],
-        name="profiles",
+    vmem = pl.BlockSpec(memory_space=pltpu.VMEM)
+    smem = pl.BlockSpec(memory_space=pltpu.SMEM)
+    anywhere = pl.BlockSpec(memory_space=pl.ANY)
+    dma = pltpu.SemaphoreType.DMA
+    table, mine = pl.pallas_call(
+        whole_kernel,
+        out_shape=(
+            jax.ShapeDtypeStruct((2 * slots, angles), jnp.bfloat16),
+            jax.ShapeDtypeStruct(shape, jnp.bfloat16),
+        ),
+        in_specs=[vmem, anywhere, smem, smem, vmem, anywhere],
+        out_specs=(vmem, vmem),
+        scratch_shapes=[
+            pltpu.VMEM((NDEV * 2 * particles, radial_rows), jnp.float32),
+            pltpu.VMEM(shape, jnp.bfloat16),
+            pltpu.VMEM(shape, jnp.bfloat16),
+            pltpu.VMEM((NDEV * 2 * particles, width), jnp.bfloat16),
+            pltpu.VMEM(shape, jnp.bfloat16),
+            pltpu.VMEM(radial_basis.shape[1:], jnp.bfloat16),
+            pltpu.VMEM((rank, width), jnp.float32),
+            *[dma] * 8,
+        ],
+        compiler_params=pltpu.CompilerParams(collective_id=0, has_side_effects=True),
+        name="whole",
+    )(
+        polar_images,
+        radial_basis,
+        radial_start,
+        radial_count,
+        order_of_slot.reshape(2, slots // 2),
+        start_block,
     )
     mine = mine.reshape(NDEV, 2, particles, radial_rows)
+    table = table.reshape(2, slots, angles)
     denoised = jnp.einsum("scpr,cst->prt", mine, table, preferred_element_type=jnp.float32)
     return denoised.astype(jnp.bfloat16)
 

time: 68.5 us -> 52.2 us (0.76)
  other arithmetic: 5.28 us -> 0 us
  local copies, waits for them, and re-layouts: 4.4 us -> 0 us
  matrix products: 6.18 us -> 2.47 us
  Pallas kernels: 51.6 us -> 49.6 us
    dot_general x3 -> x0, matrix products: 3.87 us -> none  [the longest x1 1.51 us: on_device(): jnp.einsum('cst,prt->scpr', table, polar_images, preferred_element_type=j...]
    another operation x1 -> x0, other arithmetic: 3.18 us -> none
    dynamic_slice x2 -> x0, local copies, waits for them, and re-layouts: 2.59 us -> none  [the longest x1 1.33 us: on_device(): count = lax.dynamic_index_in_dim(radial_count, slot, 0, keepdims=False)]
    pallas_call x2 -> x1, Pallas kernels: 51.6 us -> 49.6 us  [on_device(): pl.pallas_call(whole_kernel, out_shape=(jax.ShapeDtypeStruct((2 * slots,...]
    select_n x1 -> x0, other arithmetic: 1.44 us -> none  [on_device(): masked = jnp.where(keep_rows & keep_cols, basis, jnp.zeros_like(basis))]
    convert_element_type x1 -> x0, local copies, waits for them, and re-layouts: 1.2 us -> none  [on_device(): spectrum = jnp.einsum('cst,prt->scpr', table, polar_images, preferred_ele...]
where the time goes in v3:
time: 52.2 us; the launch traced here: 52.1 us
  Pallas kernels  49.6 us (95%)
  matrix products  2.47 us (5%)
    pallas_call x1, Pallas kernels, on_device(): pl.pallas_call(whole_kernel, out_shape=(jax.ShapeDtypeStruct((2 * slots,...  49.6 us
    dot_general x1, matrix products, on_device(): jnp.einsum('scpr,cst->prt', mine, table, preferred_element_type=jnp.float32)  2.47 us

profile of v3, /device:TPU:1, one launch (start us, length us, event | category | flops | bytes accessed | tf_op | source)
XLA Modules:
  0.0 52.1 jit_solution(6429747527569583829)
XLA Ops:
  0.0 49.6 %whole.1 = (bf16[512,512]{1,0:T(8,128)(2,1)}, bf16[256,8,128]{2,1,0:T(8,128)(2,1)}) custom-call(bf16[4,128,512]{2,1,0:T(8,128)(2,1)} %images_ref.1, bf16[128,128,128]{2,1,0:T(8,128)(2,1)} %radial_ref.1, s32[128]{0:T(128)} %first_ref.1, s32[128]{0:T(128)} %count_ref.1, s32[2,128]{1,0:T(2,128)} %bitcast.13, f32[128,16,128]{2,1,0:T(8,128)} %start_ref.1), custom_call_target="tpu_custom_call" | custom-call | tf_op jit(solution)/shard_map/whole/pallas_call | solution.py:221
  49.6 2.5 %fusion = bf16[4,128,512]{2,1,0:T(8,128)(2,1)} fusion(bf16[2,256,512,1]{2,1,0,3:T(8,128)(2,1)} %bitcast.11, bf16[256,2,4,128]{3,2,1,0:T(4,128)(2,1)} %bitcast.12), kind=kOutput, calls=%fused_computation.1 | convolution fusion | flops 268697600 | bytes 1572864 | tf_op jit(solution)/shard_map/scpr,cst->prt/dot_general | solution.py:251

commit v4 on v3

--- a/solution.py
+++ b/solution.py
@@ -45,45 +45,54 @@
     return out / jnp.sqrt(pivots)
 
 
-def peers():
+def place():
     d = lax.axis_index("dom")
-    o = lax.axis_index("ord")
-    z, y, x = d // (NY * NX), (d // NX) % NY, d % NX
+    return d, lax.axis_index("ord"), d // (NY * NX), (d // NX) % NY, d % NX
+
+
+def line_peers(axis):
+    d, o, z, y, x = place()
+    if axis == "z":
+        return [((z + k) % NZ * (NY * NX) + y * NX + x, o) for k in range(1, NZ)]
+    if axis == "y":
+        return [(z * (NY * NX) + (y + k) % NY * NX + x, o) for k in range(1, NY)]
+    return [(d - x + (x + k) % NX, o) for k in range(1, NX)]
+
+
+def same_core(x_offsets):
+    d, o, z, y, x = place()
     at_z = [(z + k) % NZ * (NY * NX) for k in range(NZ)]
     at_y = [(y + k) % NY * NX for k in range(NY)]
     at_x = [(x + k) % NX for k in range(NX)]
-    for dy in FAR_FIRST_4:
-        for dx in FAR_FIRST_4:
+    for dx in x_offsets:
+        for dy in FAR_FIRST_4:
             plane = at_y[dy] + at_x[dx]
             for dz in FAR_FIRST_8:
-                for other in (True, False):
-                    if other or (dz, dy, dx) != (0, 0, 0):
-                        yield at_z[dz] + plane, (1 - o if other else o)
-
-
-def greet_all():
-    barrier = pltpu.get_barrier_semaphore()
-    for pd, po in peers():
-        pl.semaphore_signal(barrier, inc=1, device_id=(pd, po), device_id_type=MESH)
-
-
-def exchange_blocks(src_ref, dst_ref, send_sem, recv_sem, own_sem):
-    d = lax.axis_index("dom")
-    o = lax.axis_index("ord")
-    mine = o * NDOM + d
-    own = pltpu.make_async_copy(src_ref.at[mine], dst_ref.at[mine], own_sem)
-    own.start()
-    for pd, po in peers():
+                if (dz, dy, dx) != (0, 0, 0):
+                    yield at_z[dz] + plane
+
+
+def greet(semaphore, devices):
+    for device in devices:
+        pl.semaphore_signal(semaphore, inc=1, device_id=device, device_id_type=MESH)
+
+
+def send_blocks(src_ref, dst_ref, send_sem, recv_sem, targets):
+    d, o = place()[:2]
+    for pd in targets:
         pltpu.make_async_remote_copy(
-            src_ref=src_ref.at[po * NDOM + pd],
-            dst_ref=dst_ref.at[mine],
+            src_ref=src_ref.at[pd],
+            dst_ref=dst_ref.at[d],
             send_sem=send_sem,
             recv_sem=recv_sem,
-            device_id=(pd, po),
+            device_id=(pd, o),
             device_id_type=MESH,
         ).start()
-    own.wait()
-    most = pl.ds(0, NDEV - 1)
+
+
+def wait_blocks(src_ref, dst_ref, send_sem, recv_sem):
+    d, o = place()[:2]
+    most = pl.ds(0, NDOM - 1)
     everything = pltpu.make_async_remote_copy(
         src_ref=src_ref.at[most],
         dst_ref=dst_ref.at[most],
@@ -94,6 +103,18 @@
     )
     everything.wait_send()
     everything.wait_recv()
+
+
+def to_sibling(src_ref, dst_ref, send_sem, recv_sem):
+    d, o = place()[:2]
+    return pltpu.make_async_remote_copy(
+        src_ref=src_ref,
+        dst_ref=dst_ref,
+        send_sem=send_sem,
+        recv_sem=recv_sem,
+        device_id=(d, 1 - o),
+        device_id_type=MESH,
+    )
 
 
 def fill_table(order_ref, table_ref):
@@ -123,17 +144,19 @@
             table_ref[256 + 128 * half : 256 + 128 * (half + 1), span] = imag.astype(jnp.bfloat16)
 
 
-def fill_spectrum(table_ref, images_ref, wide_ref, spec_ref):
-    for p in range(images_ref.shape[0]):
+def fill_spectrum(table_ref, images_ref, wide_ref):
+    slots = table_ref.shape[0] // 2
+    for p in range(0, images_ref.shape[0], 2):
+        pair = images_ref[p : p + 2].reshape(2 * images_ref.shape[1], images_ref.shape[2])
         for c in range(2):
             part = lax.dot_general(
-                table_ref[256 * c : 256 * (c + 1), :],
-                images_ref[p],
+                table_ref[slots * c : slots * (c + 1), :],
+                pair,
                 (((1,), (1,)), ((), ())),
                 preferred_element_type=jnp.float32,
             )
-            wide_ref[pl.ds(4 * c + p, NDEV, stride=8), :] = part
-    spec_ref[...] = wide_ref[...].reshape(spec_ref.shape).astype(jnp.bfloat16)
+            wide_ref[pl.ds(4 * c + p, slots, stride=8), :] = part[:, :128]
+            wide_ref[pl.ds(4 * c + p + 1, slots, stride=8), :] = part[:, 128:]
 
 
 def whole_kernel(
@@ -146,29 +169,49 @@
     table_ref,
     out_ref,
     wide_ref,
+    away_ref,
     spec_ref,
     rows_ref,
     coef_ref,
     prof_ref,
+    back_ref,
     radial_own,
     start_own,
+    send_0,
+    recv_0,
     send_1,
     recv_1,
     own_1,
     send_2,
     recv_2,
     own_2,
+    send_3,
+    recv_3,
+    own_3,
     load_1,
     load_2,
+    sem_y,
+    sem_x,
 ):
-    slot = lax.axis_index("dom")
-    greet_all()
+    slot, core = place()[:2]
+    barrier = pltpu.get_barrier_semaphore()
+    greet(barrier, line_peers("z") + line_peers("y") + line_peers("x") + [(slot, 1 - core)])
     radial_load = pltpu.make_async_copy(radial_ref.at[slot], radial_own, load_1)
     start_load = pltpu.make_async_copy(start_ref.at[slot], start_own, load_2)
     radial_load.start()
     start_load.start()
     fill_table(order_ref, table_ref)
-    fill_spectrum(table_ref, images_ref, wide_ref, spec_ref)
+    fill_spectrum(table_ref, images_ref, wide_ref)
+    half = NDOM * 8
+    away = wide_ref[pl.ds((1 - core) * half, half), :]
+    away_ref[...] = away.reshape(away_ref.shape).astype(jnp.bfloat16)
+    kept = wide_ref[pl.ds(core * half, half), :]
+    spec_ref[:, pl.ds(core, 1)] = kept.reshape(NDOM, 1, 8, kept.shape[1]).astype(jnp.bfloat16)
+
+    pl.semaphore_wait(barrier, NZ + NY + NX - 2)
+    greet(sem_y, line_peers("y"))
+    swap = to_sibling(away_ref, spec_ref.at[:, core], send_0, recv_0)
+    swap.start()
     radial_load.wait()
     start_load.wait()
     first_row = first_ref[slot] * (radial_own.shape[0] // NRB)
@@ -176,14 +219,22 @@
     col_id = lax.broadcasted_iota(jnp.int32, radial_own.shape, 1)
     keep = (row_id >= first_row) & (col_id < count_ref[slot])
     masked = jnp.where(keep, radial_own[...].astype(jnp.float32), 0.0).astype(jnp.bfloat16)
-    pl.semaphore_wait(pltpu.get_barrier_semaphore(), NDEV - 1)
-    exchange_blocks(spec_ref, rows_ref, send_1, recv_1, own_1)
+    pl.semaphore_wait(sem_y, NY - 1)
+    greet(sem_x, line_peers("x"))
+    swap.wait()
+    own = pltpu.make_async_copy(spec_ref.at[slot], rows_ref.at[slot], own_1)
+    own.start()
+    send_blocks(spec_ref, rows_ref, send_1, recv_1, same_core((0,)))
+    pl.semaphore_wait(sem_x, NX - 1)
+    send_blocks(spec_ref, rows_ref, send_1, recv_1, same_core((2, 1, 3)))
+    own.wait()
+    wait_blocks(spec_ref, rows_ref, send_1, recv_1)
 
     chunk = 512
     cov = jnp.zeros((masked.shape[1], masked.shape[1]), jnp.float32)
     for lo in range(0, coef_ref.shape[0], chunk):
-        block = rows_ref[lo // 8 : (lo + chunk) // 8].astype(jnp.float32)
-        rows = block.reshape(chunk, block.shape[2]).astype(jnp.bfloat16)
+        block = rows_ref[lo // 16 : (lo + chunk) // 16].astype(jnp.float32)
+        rows = block.reshape(chunk, block.shape[3]).astype(jnp.bfloat16)
         coef = jnp.dot(rows, masked, preferred_element_type=jnp.float32).astype(jnp.bfloat16)
         coef_ref[lo : lo + chunk, :] = coef
         cov = cov + lax.dot_general(
@@ -204,16 +255,27 @@
             preferred_element_type=jnp.float32,
         ).astype(jnp.bfloat16)
         profile = jnp.dot(scores, u_t, preferred_element_type=jnp.float32)
-        blocks = profile.reshape(chunk // 8, 8, profile.shape[1]).astype(jnp.bfloat16)
-        prof_ref[lo // 8 : (lo + chunk) // 8] = blocks
-    exchange_blocks(prof_ref, out_ref, send_2, recv_2, own_2)
+        blocks = profile.reshape(chunk // 16, 2, 8, profile.shape[1]).astype(jnp.bfloat16)
+        prof_ref[lo // 16 : (lo + chunk) // 16] = blocks
+    own = pltpu.make_async_copy(prof_ref.at[slot], back_ref.at[slot], own_2)
+    own.start()
+    send_blocks(prof_ref, back_ref, send_2, recv_2, same_core((2, 1, 3, 0)))
+    own.wait()
+    wait_blocks(prof_ref, back_ref, send_2, recv_2)
+
+    swap = to_sibling(back_ref.at[:, 1 - core], out_ref.at[core], send_3, recv_3)
+    swap.start()
+    own = pltpu.make_async_copy(back_ref.at[:, core], out_ref.at[core], own_3)
+    own.start()
+    swap.wait()
+    own.wait()
 
 
 def on_device(polar_images, radial_basis, radial_start, radial_count, order_of_slot, start_block):
     particles, radial_rows, angles = polar_images.shape
     rank, width = start_block.shape[1:]
     slots = order_of_slot.shape[0]
-    shape = (NDEV, 2 * particles, radial_rows)
+    blocks = (NDOM, 2, 2 * particles, radial_rows)
     vmem = pl.BlockSpec(memory_space=pltpu.VMEM)
     smem = pl.BlockSpec(memory_space=pltpu.SMEM)
     anywhere = pl.BlockSpec(memory_space=pl.ANY)
@@ -222,19 +284,22 @@
         whole_kernel,
         out_shape=(
             jax.ShapeDtypeStruct((2 * slots, angles), jnp.bfloat16),
-            jax.ShapeDtypeStruct(shape, jnp.bfloat16),
+            jax.ShapeDtypeStruct((2, NDOM, 2 * particles, radial_rows), jnp.bfloat16),
         ),
         in_specs=[vmem, anywhere, smem, smem, vmem, anywhere],
         out_specs=(vmem, vmem),
         scratch_shapes=[
             pltpu.VMEM((NDEV * 2 * particles, radial_rows), jnp.float32),
-            pltpu.VMEM(shape, jnp.bfloat16),
-            pltpu.VMEM(shape, jnp.bfloat16),
+            pltpu.VMEM((NDOM, 2 * particles, radial_rows), jnp.bfloat16),
+            pltpu.VMEM(blocks, jnp.bfloat16),
+            pltpu.VMEM(blocks, jnp.bfloat16),
             pltpu.VMEM((NDEV * 2 * particles, width), jnp.bfloat16),
-            pltpu.VMEM(shape, jnp.bfloat16),
+            pltpu.VMEM(blocks, jnp.bfloat16),
+            pltpu.VMEM(blocks, jnp.bfloat16),
             pltpu.VMEM(radial_basis.shape[1:], jnp.bfloat16),
             pltpu.VMEM((rank, width), jnp.float32),
-            *[dma] * 8,
+            *[dma] * 13,
+            *[pltpu.SemaphoreType.REGULAR] * 2,
         ],
         compiler_params=pltpu.CompilerParams(collective_id=0, has_side_effects=True),
         name="whole",

time: 52.2 us -> 51.4 us (0.985)
  Pallas kernels: 49.6 us -> 48.9 us
    pallas_call x1, Pallas kernels: 49.6 us -> 48.9 us  [on_device(): pl.pallas_call(whole_kernel, out_shape=(jax.ShapeDtypeStruct((2 * slots,...]
where the time goes in v4:
time: 51.4 us; the launch traced here: 51.3 us
  Pallas kernels  48.9 us (95%)
  matrix products  2.47 us (5%)
    pallas_call x1, Pallas kernels, on_device(): pl.pallas_call(whole_kernel, out_shape=(jax.ShapeDtypeStruct((2 * slots,...  48.9 us
    dot_general x1, matrix products, on_device(): jnp.einsum('scpr,cst->prt', mine, table, preferred_element_type=jnp.float32)  2.47 us

profile of v4, /device:TPU:1, one launch (start us, length us, event | category | flops | bytes accessed | tf_op | source)
XLA Modules:
  0.0 51.3 jit_solution(3989130995804329395)
XLA Ops:
  0.0 48.9 %whole.1 = (bf16[512,512]{1,0:T(8,128)(2,1)}, bf16[2,128,8,128]{3,2,1,0:T(8,128)(2,1)}) custom-call(bf16[4,128,512]{2,1,0:T(8,128)(2,1)} %images_ref.1, bf16[128,128,128]{2,1,0:T(8,128)(2,1)} %radial_ref.1, s32[128]{0:T(128)} %first_ref.1, s32[128]{0:T(128)} %count_ref.1, s32[2,128]{1,0:T(2,128)} %bitcast.13, f32[128,16,128]{2,1,0:T(8,128)} %start_ref.1), custom_call_target="tpu_custom_call" | custom-call | tf_op jit(solution)/shard_map/whole/pallas_call | solution.py:283
  48.9 2.5 %fusion = bf16[4,128,512]{2,1,0:T(8,128)(2,1)} fusion(bf16[2,256,512,1]{2,1,0,3:T(8,128)(2,1)} %bitcast.11, bf16[256,2,4,128]{3,2,1,0:T(4,128)(2,1)} %bitcast.12), kind=kOutput, calls=%fused_computation.1 | convolution fusion | flops 268697600 | bytes 1572864 | tf_op jit(solution)/shard_map/scpr,cst->prt/dot_general | solution.py:316

commit v5 on v3

v5 whole, which is shorter than its diff:
```python
import math

import jax
import jax.numpy as jnp
from jax import lax
from jax.experimental import pallas as pl
from jax.experimental.pallas import tpu as pltpu
from jax.sharding import PartitionSpec as P

NRB = 8
ITERS = 4
NZ, NY, NX = 8, 4, 4
NDOM = NZ * NY * NX
NPLANE = 2 * NY * NX
MESH = pl.DeviceIdType.MESH


FAR_FIRST_8 = (4, 3, 5, 2, 6, 1, 7, 0)
FAR_FIRST_4 = (2, 1, 3, 0)


def dot32(a, b, dims):
    return lax.dot_general(
        a, b, (dims, ((), ())), precision=lax.Precision.HIGHEST, preferred_element_type=jnp.float32
    )


def orthonormal(image_t):
    rank, width = image_t.shape
    gram = dot32(image_t, image_t, ((1,), (1,)))
    lane_block = lax.broadcasted_iota(jnp.int32, (rank, rank * width), 1) // width
    spread = lane_block == lax.broadcasted_iota(jnp.int32, (rank, rank * width), 0)
    wide = dot32(gram, spread.astype(jnp.float32), ((1,), (0,)))
    cols = [wide[:, j * width : (j + 1) * width] for j in range(rank)]
    row_id = lax.broadcasted_iota(jnp.int32, (rank, width), 0)
    pivots = jnp.ones((rank, width), jnp.float32)
    out = image_t
    for j in range(rank):
        pivot = jnp.broadcast_to(cols[j][j : j + 1, :], (rank, width))
        pivots = jnp.where(row_id == j, pivot, pivots)
        factor = jnp.where(row_id > j, cols[j] / pivot, 0.0)
        for k in range(j + 1, rank):
            cols[k] = cols[k] - factor * cols[k][j : j + 1, :]
        out = out - factor * out[j : j + 1, :]
    return out / jnp.sqrt(pivots)


def place():
    d = lax.axis_index("dom")
    return d, lax.axis_index("ord"), d // (NY * NX), (d // NX) % NY, d % NX


def z_peers():
    d, o, z, y, x = place()
    for k in FAR_FIRST_8[:-1]:
        pz = (z + k) % NZ
        yield pz, pz * (NY * NX) + y * NX + x


def plane_peers():
    d, o, z, y, x = place()
    at_y = [(y + k) % NY * NX for k in range(NY)]
    at_x = [(x + k) % NX for k in range(NX)]
    for dy in FAR_FIRST_4:
        for dx in FAR_FIRST_4:
            m = at_y[dy] + at_x[dx]
            for po in (1 - o, o) if (dy, dx) != (0, 0) else (1 - o,):
                yield po * (NY * NX) + m, z * (NY * NX) + m, po


def remote(src_ref, dst_ref, send_sem, recv_sem, device):
    return pltpu.make_async_remote_copy(
        src_ref=src_ref,
        dst_ref=dst_ref,
        send_sem=send_sem,
        recv_sem=recv_sem,
        device_id=device,
        device_id_type=MESH,
    )


def wait_blocks(src_ref, dst_ref, send_sem, recv_sem, blocks):
    d, o = place()[:2]
    most = pl.ds(0, blocks)
    everything = remote(src_ref.at[most], dst_ref.at[most], send_sem, recv_sem, (d, 1 - o))
    everything.wait_send()
    everything.wait_recv()


def plane_exchange(src_ref, dst_ref, send_sem, recv_sem, own_sem):
    d, o, z, y, x = place()
    mine = o * (NY * NX) + y * NX + x
    for index, pd, po in plane_peers():
        remote(src_ref.at[index], dst_ref.at[mine], send_sem, recv_sem, (pd, po)).start()
    own = pltpu.make_async_copy(src_ref.at[mine], dst_ref.at[mine], own_sem)
    own.start()
    own.wait()
    wait_blocks(src_ref, dst_ref, send_sem, recv_sem, NPLANE - 1)


def fill_table(order_ref, table_ref):
    angles = table_ref.shape[1]
    weight = math.sqrt(2.0 / angles)
    for half in range(2):
        row = order_ref[half : half + 1, :].astype(jnp.float32)
        k = jnp.broadcast_to(row, (128, 128)).T.astype(jnp.int32)
        lane = lax.broadcasted_iota(jnp.int32, (128, 128), 1)
        turn = (k * lane) & (angles - 1)
        quarter = (turn + angles // 8) >> 7
        angle = (turn - quarter * (angles // 4)).astype(jnp.float32) * (2.0 * math.pi / angles)
        sq = angle * angle
        cos = 1.0 + sq * (-1 / 2 + sq * (1 / 24 + sq * (-1 / 720 + sq * (1 / 40320))))
        sin = angle * (1.0 + sq * (-1 / 6 + sq * (1 / 120 + sq * (-1 / 5040 + sq * (1 / 362880)))))
        cos = cos * weight
        sin = sin * weight
        for b in range(angles // 128):
            quadrant = (quarter + b * k) & 3
            odd = (quadrant & 1) == 1
            upper = quadrant >= 2
            even_sign = jnp.where(upper, -1.0, 1.0)
            real = jnp.where(odd, -sin, cos) * even_sign
            imag = jnp.where(odd, -cos, -sin) * even_sign
            span = slice(128 * b, 128 * (b + 1))
            table_ref[128 * half : 128 * (half + 1), span] = real.astype(jnp.bfloat16)
            table_ref[256 + 128 * half : 256 + 128 * (half + 1), span] = imag.astype(jnp.bfloat16)


def fill_spectrum(table_ref, images_ref, wide_ref):
    slots = table_ref.shape[0] // 2
    for p in range(0, images_ref.shape[0], 2):
        pair = images_ref[p : p + 2].reshape(2 * images_ref.shape[1], images_ref.shape[2])
        for c in range(2):
            part = lax.dot_general(
                table_ref[slots * c : slots * (c + 1), :],
                pair,
                (((1,), (1,)), ((), ())),
                preferred_element_type=jnp.float32,
            )
            wide_ref[pl.ds(4 * c + p, slots, stride=8), :] = part[:, :128]
            wide_ref[pl.ds(4 * c + p + 1, slots, stride=8), :] = part[:, 128:]


def whole_kernel(
    images_ref,
    radial_ref,
    first_ref,
    count_ref,
    order_ref,
    start_ref,
    table_ref,
    out_ref,
    wide_ref,
    spec_ref,
    rows_ref,
    masked_ref,
    coef_ref,
    part_ref,
    given_ref,
    taken_ref,
    eig_ref,
    eigs_ref,
    prof_ref,
    start_own,
    send_1,
    recv_1,
    own_1,
    send_2,
    recv_2,
    send_3,
    recv_3,
    send_4,
    recv_4,
    own_4,
    load_1,
    load_2,
):
    d, o, z, y, x = place()
    first_slot = (y * NX + x) * NZ
    barrier = pltpu.get_barrier_semaphore()
    for _, pd in z_peers():
        pl.semaphore_signal(barrier, inc=1, device_id=(pd, o), device_id_type=MESH)
    for _, pd, po in plane_peers():
        pl.semaphore_signal(barrier, inc=1, device_id=(pd, po), device_id_type=MESH)
    radial_load = pltpu.make_async_copy(radial_ref.at[pl.ds(first_slot, NZ)], masked_ref, load_1)
    start_load = pltpu.make_async_copy(start_ref.at[first_slot + z], start_own, load_2)
    radial_load.start()
    start_load.start()
    fill_table(order_ref, table_ref)
    fill_spectrum(table_ref, images_ref, wide_ref)
    spec_ref[...] = wide_ref[...].reshape(spec_ref.shape).astype(jnp.bfloat16)
    radial_load.wait()
    start_load.wait()
    radial_rows, width = masked_ref.shape[1:]
    row_id = lax.broadcasted_iota(jnp.int32, (radial_rows, width), 0)
    col_id = lax.broadcasted_iota(jnp.int32, (radial_rows, width), 1)
    for j in range(NZ):
        first_row = first_ref[first_slot + j] * (radial_rows // NRB)
        keep = (row_id >= first_row) & (col_id < count_ref[first_slot + j])
        masked = jnp.where(keep, masked_ref[j].astype(jnp.float32), 0.0)
        masked_ref[j] = masked.astype(jnp.bfloat16)
    pl.semaphore_wait(barrier, NPLANE - 1 + NZ - 1)
    plane_exchange(spec_ref, rows_ref, send_1, recv_1, own_1)

    waiting = None
    for j, pd in [*z_peers(), (z, None)]:
        rows = rows_ref[:, j].astype(jnp.float32).reshape(NPLANE * 8, radial_rows).astype(jnp.bfloat16)
        coef = jnp.dot(rows, masked_ref[j], preferred_element_type=jnp.float32).astype(jnp.bfloat16)
        coef_ref[j] = coef
        part = lax.dot_general(
            coef, coef, (((0,), (0,)), ((), ())), preferred_element_type=jnp.float32
        )
        if pd is not None:
            given_ref[j] = part.astype(jnp.bfloat16)
        if waiting is not None:
            waiting.start()
        if pd is not None:
            waiting = remote(given_ref.at[j], taken_ref.at[z], send_2, recv_2, (pd, o))
    part_ref[...] = part
    wait_blocks(given_ref, taken_ref, send_2, recv_2, NZ - 1)
    cov = part_ref[...]
    for k in range(1, NZ):
        cov = cov + taken_ref[(z + k) % NZ].astype(jnp.float32)

    basis_t = start_own[...]
    for step in range(ITERS):
        basis_t = orthonormal(dot32(basis_t, cov, ((1,), (0,))))
    eig_t = basis_t.astype(jnp.bfloat16)
    eig_ref[...] = eig_t
    eigs_ref[z] = eig_t
    for _, pd in z_peers():
        remote(eig_ref, eigs_ref.at[z], send_3, recv_3, (pd, o)).start()
    wait_blocks(eigs_ref, eigs_ref, send_3, recv_3, NZ - 1)

    for j in range(NZ):
        eig_t = eigs_ref[j]
        u_t = lax.dot_general(
            eig_t, masked_ref[j], (((1,), (1,)), ((), ())), preferred_element_type=jnp.float32
        ).astype(jnp.bfloat16)
        scores = lax.dot_general(
            coef_ref[j], eig_t, (((1,), (1,)), ((), ())), preferred_element_type=jnp.float32
        ).astype(jnp.bfloat16)
        profile = jnp.dot(scores, u_t, preferred_element_type=jnp.float32)
        prof_ref[:, j] = profile.reshape(NPLANE, 8, radial_rows).astype(jnp.bfloat16)
    plane_exchange(prof_ref, out_ref, send_4, recv_4, own_4)


def on_device(polar_images, radial_basis, radial_start, radial_count, order_of_slot, start_block):
    particles, radial_rows, angles = polar_images.shape
    rank, width = start_block.shape[1:]
    slots = order_of_slot.shape[0]
    blocks = (NPLANE, NZ, 2 * particles, radial_rows)
    vmem = pl.BlockSpec(memory_space=pltpu.VMEM)
    smem = pl.BlockSpec(memory_space=pltpu.SMEM)
    anywhere = pl.BlockSpec(memory_space=pl.ANY)
    table, mine = pl.pallas_call(
        whole_kernel,
        out_shape=(
            jax.ShapeDtypeStruct((2 * slots, angles), jnp.bfloat16),
            jax.ShapeDtypeStruct(blocks, jnp.bfloat16),
        ),
        in_specs=[vmem, anywhere, smem, smem, vmem, anywhere],
        out_specs=(vmem, vmem),
        scratch_shapes=[
            pltpu.VMEM((slots * 2 * particles, radial_rows), jnp.float32),
            pltpu.VMEM(blocks, jnp.bfloat16),
            pltpu.VMEM(blocks, jnp.bfloat16),
            pltpu.VMEM((NZ, radial_rows, width), jnp.bfloat16),
            pltpu.VMEM((NZ, NPLANE * 2 * particles, width), jnp.bfloat16),
            pltpu.VMEM((width, width), jnp.float32),
            pltpu.VMEM((NZ, width, width), jnp.bfloat16),
            pltpu.VMEM((NZ, width, width), jnp.bfloat16),
            pltpu.VMEM((rank, width), jnp.bfloat16),
            pltpu.VMEM((NZ, rank, width), jnp.bfloat16),
            pltpu.VMEM(blocks, jnp.bfloat16),
            pltpu.VMEM((rank, width), jnp.float32),
            *[pltpu.SemaphoreType.DMA] * 12,
        ],
        compiler_params=pltpu.CompilerParams(collective_id=0, has_side_effects=True),
        name="whole",
    )(
        polar_images,
        radial_basis,
        radial_start,
        radial_count,
        order_of_slot.reshape(2, slots // 2),
        start_block,
    )
    mine = mine.reshape(slots, 2, particles, radial_rows)
    table = table.reshape(2, slots, angles)
    denoised = jnp.einsum("scpr,cst->prt", mine, table, preferred_element_type=jnp.float32)
    return denoised.astype(jnp.bfloat16)


def solution(mesh):
    placed = (
        P(("dom", "ord"), None, None),
        P("ord", None, None),
        P("ord"),
        P("ord"),
        P(),
        P("ord", None, None),
    )
    return jax.shard_map(
        on_device,
        mesh=mesh,
        in_specs=placed,
        out_specs=P(("dom", "ord"), None, None),
        check_vma=False,
    )
```

time: 52.2 us -> 47.5 us (0.910)
  Pallas kernels: 49.6 us -> 44.9 us
    pallas_call x1, Pallas kernels: 49.6 us -> 44.9 us  [on_device(): pl.pallas_call(whole_kernel, out_shape=(jax.ShapeDtypeStruct((2 * slots,...]
where the time goes in v5:
time: 47.5 us; the launch traced here: 47.4 us
  Pallas kernels  44.9 us (95%)
  matrix products  2.47 us (5%)
    pallas_call x1, Pallas kernels, on_device(): pl.pallas_call(whole_kernel, out_shape=(jax.ShapeDtypeStruct((2 * slots,...  44.9 us
    dot_general x1, matrix products, on_device(): jnp.einsum('scpr,cst->prt', mine, table, preferred_element_type=jnp.float32)  2.47 us

profile of v5, /device:TPU:1, one launch (start us, length us, event | category | flops | bytes accessed | tf_op | source)
XLA Modules:
  0.0 47.4 jit_solution(17103289958317147422)
XLA Ops:
  0.0 44.9 %whole.1 = (bf16[512,512]{1,0:T(8,128)(2,1)}, bf16[32,8,8,128]{3,2,1,0:T(8,128)(2,1)}) custom-call(bf16[4,128,512]{2,1,0:T(8,128)(2,1)} %images_ref.1, bf16[128,128,128]{2,1,0:T(8,128)(2,1)} %radial_ref.1, s32[128]{0:T(128)} %first_ref.1, s32[128]{0:T(128)} %count_ref.1, s32[2,128]{1,0:T(2,128)} %bitcast.13, f32[128,16,128]{2,1,0:T(8,128)} %start_ref.1), custom_call_target="tpu_custom_call" | custom-call | tf_op jit(solution)/shard_map/whole/pallas_call | solution.py:255
  44.9 2.5 %fusion = bf16[4,128,512]{2,1,0:T(8,128)(2,1)} fusion(bf16[2,256,512,1]{2,1,0,3:T(8,128)(2,1)} %bitcast.11, bf16[256,2,4,128]{3,2,1,0:T(4,128)(2,1)} %bitcast.12), kind=kOutput, calls=%fused_computation.1 | convolution fusion | flops 268697600 | bytes 1572864 | tf_op jit(solution)/shard_map/scpr,cst->prt/dot_general | solution.py:290

commit v6 on v5

--- a/solution.py
+++ b/solution.py
@@ -17,6 +17,7 @@
 
 FAR_FIRST_8 = (4, 3, 5, 2, 6, 1, 7, 0)
 FAR_FIRST_4 = (2, 1, 3, 0)
+SLOT_PARTS = ((0, 1, 2, 3), (4, 5, 6, 7))
 
 
 def dot32(a, b, dims):
@@ -187,7 +188,11 @@
     start_load.start()
     fill_table(order_ref, table_ref)
     fill_spectrum(table_ref, images_ref, wide_ref)
-    spec_ref[...] = wide_ref[...].reshape(spec_ref.shape).astype(jnp.bfloat16)
+    by_slot = wide_ref.reshape(NPLANE, NZ * 8, wide_ref.shape[1])
+    for i, k in enumerate(FAR_FIRST_8):
+        j = (z + k) % NZ
+        slot_rows = by_slot[:, pl.ds(pl.multiple_of(j * 8, 8), 8), :]
+        spec_ref[:, i] = slot_rows.astype(jnp.bfloat16)
     radial_load.wait()
     start_load.wait()
     radial_rows, width = masked_ref.shape[1:]
@@ -199,11 +204,34 @@
         masked = jnp.where(keep, masked_ref[j].astype(jnp.float32), 0.0)
         masked_ref[j] = masked.astype(jnp.bfloat16)
     pl.semaphore_wait(barrier, NPLANE - 1 + NZ - 1)
-    plane_exchange(spec_ref, rows_ref, send_1, recv_1, own_1)
+    mine = o * (NY * NX) + y * NX + x
+    own = pltpu.make_async_copy(spec_ref.at[mine], rows_ref.at[mine], own_1)
+    own.start()
+    for part_id, slots in enumerate(SLOT_PARTS):
+        span = pl.ds(slots[0], len(slots))
+        for index, pd, po in plane_peers():
+            remote(
+                spec_ref.at[index, span],
+                rows_ref.at[mine, span],
+                send_1.at[part_id],
+                recv_1.at[part_id],
+                (pd, po),
+            ).start()
+    own.wait()
 
     waiting = None
-    for j, pd in [*z_peers(), (z, None)]:
-        rows = rows_ref[:, j].astype(jnp.float32).reshape(NPLANE * 8, radial_rows).astype(jnp.bfloat16)
+    for i, (j, pd) in enumerate([*z_peers(), (z, None)]):
+        for part_id, slots in enumerate(SLOT_PARTS):
+            if i == slots[0]:
+                span = pl.ds(slots[0], len(slots))
+                wait_blocks(
+                    spec_ref.at[:, span],
+                    rows_ref.at[:, span],
+                    send_1.at[part_id],
+                    recv_1.at[part_id],
+                    NPLANE - 1,
+                )
+        rows = rows_ref[:, i].astype(jnp.float32).reshape(NPLANE * 8, radial_rows).astype(jnp.bfloat16)
         coef = jnp.dot(rows, masked_ref[j], preferred_element_type=jnp.float32).astype(jnp.bfloat16)
         coef_ref[j] = coef
         part = lax.dot_general(
@@ -273,7 +301,8 @@
             pltpu.VMEM((NZ, rank, width), jnp.bfloat16),
             pltpu.VMEM(blocks, jnp.bfloat16),
             pltpu.VMEM((rank, width), jnp.float32),
-            *[pltpu.SemaphoreType.DMA] * 12,
+            *[pltpu.SemaphoreType.DMA((len(SLOT_PARTS),))] * 2,
+            *[pltpu.SemaphoreType.DMA] * 10,
         ],
         compiler_params=pltpu.CompilerParams(collective_id=0, has_side_effects=True),
         name="whole",

time: 47.5 us -> 46.4 us (0.977)
  Pallas kernels: 44.9 us -> 43.8 us
    pallas_call x1, Pallas kernels: 44.9 us -> 43.8 us  [on_device(): pl.pallas_call(whole_kernel, out_shape=(jax.ShapeDtypeStruct((2 * slots,...]
where the time goes in v6:
time: 46.4 us; the launch traced here: 46.2 us
  Pallas kernels  43.8 us (94%)
  matrix products  2.47 us (5%)
    pallas_call x1, Pallas kernels, on_device(): pl.pallas_call(whole_kernel, out_shape=(jax.ShapeDtypeStruct((2 * slots,...  43.8 us
    dot_general x1, matrix products, on_device(): jnp.einsum('scpr,cst->prt', mine, table, preferred_element_type=jnp.float32)  2.47 us

profile of v6, /device:TPU:1, one launch (start us, length us, event | category | flops | bytes accessed | tf_op | source)
XLA Modules:
  0.0 46.2 jit_solution(7036058669141795741)
XLA Ops:
  0.0 43.8 %whole.1 = (bf16[512,512]{1,0:T(8,128)(2,1)}, bf16[32,8,8,128]{3,2,1,0:T(8,128)(2,1)}) custom-call(bf16[4,128,512]{2,1,0:T(8,128)(2,1)} %images_ref.1, bf16[128,128,128]{2,1,0:T(8,128)(2,1)} %radial_ref.1, s32[128]{0:T(128)} %first_ref.1, s32[128]{0:T(128)} %count_ref.1, s32[2,128]{1,0:T(2,128)} %bitcast.13, f32[128,16,128]{2,1,0:T(8,128)} %start_ref.1), custom_call_target="tpu_custom_call" | custom-call | tf_op jit(solution)/shard_map/whole/pallas_call | solution.py:283
  43.8 2.5 %fusion = bf16[4,128,512]{2,1,0:T(8,128)(2,1)} fusion(bf16[2,256,512,1]{2,1,0,3:T(8,128)(2,1)} %bitcast.11, bf16[256,2,4,128]{3,2,1,0:T(4,128)(2,1)} %bitcast.12), kind=kOutput, calls=%fused_computation.1 | convolution fusion | flops 268697600 | bytes 1572864 | tf_op jit(solution)/shard_map/scpr,cst->prt/dot_general | solution.py:319

commit v7 on v5

--- a/solution.py
+++ b/solution.py
@@ -17,6 +17,7 @@
 
 FAR_FIRST_8 = (4, 3, 5, 2, 6, 1, 7, 0)
 FAR_FIRST_4 = (2, 1, 3, 0)
+SLOT_PARTS = ((0, 1), (2, 3), (4, 5), (6, 7))
 
 
 def dot32(a, b, dims):
@@ -52,9 +53,9 @@
 
 def z_peers():
     d, o, z, y, x = place()
-    for k in FAR_FIRST_8[:-1]:
-        pz = (z + k) % NZ
-        yield pz, pz * (NY * NX) + y * NX + x
+    for i, k in enumerate(FAR_FIRST_8[:-1]):
+        pd = (z + k) % NZ * (NY * NX) + y * NX + x
+        yield i, FAR_FIRST_8.index((NZ - k) % NZ), pd
 
 
 def plane_peers():
@@ -87,24 +88,52 @@
     everything.wait_recv()
 
 
-def plane_exchange(src_ref, dst_ref, send_sem, recv_sem, own_sem):
+def own_block(src_ref, dst_ref, own_sem):
     d, o, z, y, x = place()
     mine = o * (NY * NX) + y * NX + x
+    return pltpu.make_async_copy(src_ref.at[mine], dst_ref.at[mine], own_sem)
+
+
+def send_part(part, src_ref, dst_ref, send_sem, recv_sem):
+    d, o, z, y, x = place()
+    mine = o * (NY * NX) + y * NX + x
+    span = pl.ds(SLOT_PARTS[part][0], len(SLOT_PARTS[part]))
     for index, pd, po in plane_peers():
-        remote(src_ref.at[index], dst_ref.at[mine], send_sem, recv_sem, (pd, po)).start()
-    own = pltpu.make_async_copy(src_ref.at[mine], dst_ref.at[mine], own_sem)
-    own.start()
-    own.wait()
-    wait_blocks(src_ref, dst_ref, send_sem, recv_sem, NPLANE - 1)
+        remote(
+            src_ref.at[index, span],
+            dst_ref.at[mine, span],
+            send_sem.at[part],
+            recv_sem.at[part],
+            (pd, po),
+        ).start()
+
+
+def wait_part(part, src_ref, dst_ref, send_sem, recv_sem):
+    span = pl.ds(SLOT_PARTS[part][0], len(SLOT_PARTS[part]))
+    wait_blocks(
+        src_ref.at[:, span], dst_ref.at[:, span], send_sem.at[part], recv_sem.at[part], NPLANE - 1
+    )
 
 
 def fill_table(order_ref, table_ref):
     angles = table_ref.shape[1]
     weight = math.sqrt(2.0 / angles)
+    z = place()[2]
+    row_id = lax.broadcasted_iota(jnp.int32, (128, 128), 0)
+    lane = lax.broadcasted_iota(jnp.int32, (128, 128), 1)
+    spot = row_id & (NZ - 1)
+    step = (spot + 1) >> 1
+    offset = NZ // 2 + jnp.where((spot & 1) == 1, -step, step)
+    chosen = lane == row_id - spot + ((z + offset) & (NZ - 1))
+    chosen = jnp.where(chosen, 1.0, 0.0).astype(jnp.bfloat16)
     for half in range(2):
         row = order_ref[half : half + 1, :].astype(jnp.float32)
-        k = jnp.broadcast_to(row, (128, 128)).T.astype(jnp.int32)
-        lane = lax.broadcasted_iota(jnp.int32, (128, 128), 1)
+        k = lax.dot_general(
+            chosen,
+            jnp.broadcast_to(row, (128, 128)).astype(jnp.bfloat16),
+            (((1,), (1,)), ((), ())),
+            preferred_element_type=jnp.float32,
+        ).astype(jnp.int32)
         turn = (k * lane) & (angles - 1)
         quarter = (turn + angles // 8) >> 7
         angle = (turn - quarter * (angles // 4)).astype(jnp.float32) * (2.0 * math.pi / angles)
@@ -152,24 +181,24 @@
     wide_ref,
     spec_ref,
     rows_ref,
+    radial_own,
     masked_ref,
     coef_ref,
     part_ref,
     given_ref,
     taken_ref,
-    eig_ref,
     eigs_ref,
     prof_ref,
     start_own,
     send_1,
     recv_1,
-    own_1,
+    send_4,
+    recv_4,
+    send_3,
+    recv_3,
     send_2,
     recv_2,
-    send_3,
-    recv_3,
-    send_4,
-    recv_4,
+    own_1,
     own_4,
     load_1,
     load_2,
@@ -177,11 +206,11 @@
     d, o, z, y, x = place()
     first_slot = (y * NX + x) * NZ
     barrier = pltpu.get_barrier_semaphore()
-    for _, pd in z_peers():
+    for _, _, pd in z_peers():
         pl.semaphore_signal(barrier, inc=1, device_id=(pd, o), device_id_type=MESH)
     for _, pd, po in plane_peers():
         pl.semaphore_signal(barrier, inc=1, device_id=(pd, po), device_id_type=MESH)
-    radial_load = pltpu.make_async_copy(radial_ref.at[pl.ds(first_slot, NZ)], masked_ref, load_1)
+    radial_load = pltpu.make_async_copy(radial_ref.at[pl.ds(first_slot, NZ)], radial_own, load_1)
     start_load = pltpu.make_async_copy(start_ref.at[first_slot + z], start_own, load_2)
     radial_load.start()
     start_load.start()
@@ -193,55 +222,81 @@
     radial_rows, width = masked_ref.shape[1:]
     row_id = lax.broadcasted_iota(jnp.int32, (radial_rows, width), 0)
     col_id = lax.broadcasted_iota(jnp.int32, (radial_rows, width), 1)
-    for j in range(NZ):
+    for i, k in enumerate(FAR_FIRST_8):
+        j = (z + k) % NZ
         first_row = first_ref[first_slot + j] * (radial_rows // NRB)
         keep = (row_id >= first_row) & (col_id < count_ref[first_slot + j])
-        masked = jnp.where(keep, masked_ref[j].astype(jnp.float32), 0.0)
-        masked_ref[j] = masked.astype(jnp.bfloat16)
+        masked = jnp.where(keep, radial_own[j].astype(jnp.float32), 0.0)
+        masked_ref[i] = masked.astype(jnp.bfloat16)
     pl.semaphore_wait(barrier, NPLANE - 1 + NZ - 1)
-    plane_exchange(spec_ref, rows_ref, send_1, recv_1, own_1)
-
+    own = own_block(spec_ref, rows_ref, own_1)
+    own.start()
+    for part in range(len(SLOT_PARTS)):
+        send_part(part, spec_ref, rows_ref, send_1, recv_1)
+    own.wait()
+
+    peers = list(z_peers())
     waiting = None
-    for j, pd in [*z_peers(), (z, None)]:
-        rows = rows_ref[:, j].astype(jnp.float32).reshape(NPLANE * 8, radial_rows).astype(jnp.bfloat16)
-        coef = jnp.dot(rows, masked_ref[j], preferred_element_type=jnp.float32).astype(jnp.bfloat16)
-        coef_ref[j] = coef
-        part = lax.dot_general(
-            coef, coef, (((0,), (0,)), ((), ())), preferred_element_type=jnp.float32
-        )
-        if pd is not None:
-            given_ref[j] = part.astype(jnp.bfloat16)
-        if waiting is not None:
-            waiting.start()
-        if pd is not None:
-            waiting = remote(given_ref.at[j], taken_ref.at[z], send_2, recv_2, (pd, o))
-    part_ref[...] = part
+    for part, spots in enumerate(SLOT_PARTS):
+        wait_part(part, spec_ref, rows_ref, send_1, recv_1)
+        for i in spots:
+            rows = rows_ref[:, i].astype(jnp.float32).reshape(NPLANE * 8, radial_rows)
+            coef = jnp.dot(
+                rows.astype(jnp.bfloat16), masked_ref[i], preferred_element_type=jnp.float32
+            ).astype(jnp.bfloat16)
+            coef_ref[i] = coef
+            cov = lax.dot_general(
+                coef, coef, (((0,), (0,)), ((), ())), preferred_element_type=jnp.float32
+            )
+            if i < len(peers):
+                given_ref[i] = cov.astype(jnp.bfloat16)
+            else:
+                part_ref[...] = cov
+            if waiting is not None:
+                waiting.start()
+            if i < len(peers):
+                _, there, pd = peers[i]
+                waiting = remote(given_ref.at[i], taken_ref.at[there], send_2, recv_2, (pd, o))
     wait_blocks(given_ref, taken_ref, send_2, recv_2, NZ - 1)
     cov = part_ref[...]
-    for k in range(1, NZ):
-        cov = cov + taken_ref[(z + k) % NZ].astype(jnp.float32)
+    for i in range(NZ - 1):
+        cov = cov + taken_ref[i].astype(jnp.float32)
 
     basis_t = start_own[...]
     for step in range(ITERS):
         basis_t = orthonormal(dot32(basis_t, cov, ((1,), (0,))))
     eig_t = basis_t.astype(jnp.bfloat16)
-    eig_ref[...] = eig_t
-    eigs_ref[z] = eig_t
-    for _, pd in z_peers():
-        remote(eig_ref, eigs_ref.at[z], send_3, recv_3, (pd, o)).start()
-    wait_blocks(eigs_ref, eigs_ref, send_3, recv_3, NZ - 1)
-
-    for j in range(NZ):
-        eig_t = eigs_ref[j]
-        u_t = lax.dot_general(
-            eig_t, masked_ref[j], (((1,), (1,)), ((), ())), preferred_element_type=jnp.float32
-        ).astype(jnp.bfloat16)
-        scores = lax.dot_general(
-            coef_ref[j], eig_t, (((1,), (1,)), ((), ())), preferred_element_type=jnp.float32
-        ).astype(jnp.bfloat16)
-        profile = jnp.dot(scores, u_t, preferred_element_type=jnp.float32)
-        prof_ref[:, j] = profile.reshape(NPLANE, 8, radial_rows).astype(jnp.bfloat16)
-    plane_exchange(prof_ref, out_ref, send_4, recv_4, own_4)
+    eigs_ref[NZ - 1] = eig_t
+    for i, there, pd in peers:
+        remote(
+            eigs_ref.at[NZ - 1], eigs_ref.at[there], send_3.at[i], recv_3.at[there], (pd, o)
+        ).start()
+
+    for part in reversed(range(len(SLOT_PARTS))):
+        for i in reversed(SLOT_PARTS[part]):
+            if i < len(peers):
+                remote(
+                    eigs_ref.at[i], eigs_ref.at[i], send_3.at[i], recv_3.at[i], (peers[i][2], o)
+                ).wait_recv()
+            eig_t = eigs_ref[i]
+            u_t = lax.dot_general(
+                eig_t, masked_ref[i], (((1,), (1,)), ((), ())), preferred_element_type=jnp.float32
+            ).astype(jnp.bfloat16)
+            scores = lax.dot_general(
+                coef_ref[i], eig_t, (((1,), (1,)), ((), ())), preferred_element_type=jnp.float32
+            ).astype(jnp.bfloat16)
+            profile = jnp.dot(scores, u_t, preferred_element_type=jnp.float32)
+            prof_ref[:, i] = profile.reshape(NPLANE, 8, radial_rows).astype(jnp.bfloat16)
+        send_part(part, prof_ref, out_ref, send_4, recv_4)
+    own = own_block(prof_ref, out_ref, own_4)
+    own.start()
+    for i, _, pd in peers:
+        remote(
+            eigs_ref.at[NZ - 1], eigs_ref.at[i], send_3.at[i], recv_3.at[i], (pd, o)
+        ).wait_send()
+    own.wait()
+    for part in reversed(range(len(SLOT_PARTS))):
+        wait_part(part, prof_ref, out_ref, send_4, recv_4)
 
 
 def on_device(polar_images, radial_basis, radial_start, radial_count, order_of_slot, start_block):
@@ -265,15 +320,17 @@
             pltpu.VMEM(blocks, jnp.bfloat16),
             pltpu.VMEM(blocks, jnp.bfloat16),
             pltpu.VMEM((NZ, radial_rows, width), jnp.bfloat16),
+            pltpu.VMEM((NZ, radial_rows, width), jnp.bfloat16),
             pltpu.VMEM((NZ, NPLANE * 2 * particles, width), jnp.bfloat16),
             pltpu.VMEM((width, width), jnp.float32),
             pltpu.VMEM((NZ, width, width), jnp.bfloat16),
             pltpu.VMEM((NZ, width, width), jnp.bfloat16),
-            pltpu.VMEM((rank, width), jnp.bfloat16),
             pltpu.VMEM((NZ, rank, width), jnp.bfloat16),
             pltpu.VMEM(blocks, jnp.bfloat16),
             pltpu.VMEM((rank, width), jnp.float32),
-            *[pltpu.SemaphoreType.DMA] * 12,
+            *[pltpu.SemaphoreType.DMA((len(SLOT_PARTS),))] * 4,
+            *[pltpu.SemaphoreType.DMA((NZ - 1,))] * 2,
+            *[pltpu.SemaphoreType.DMA] * 6,
         ],
         compiler_params=pltpu.CompilerParams(collective_id=0, has_side_effects=True),
         name="whole",

time: 47.5 us -> 44.4 us (0.935)
  Pallas kernels: 44.9 us -> 41.8 us
    pallas_call x1, Pallas kernels: 44.9 us -> 41.8 us  [on_device(): pl.pallas_call(whole_kernel, out_shape=(jax.ShapeDtypeStruct((2 * slots,...]
where the time goes in v7:
time: 44.4 us; the launch traced here: 44.3 us
  Pallas kernels  41.8 us (94%)
  matrix products  2.47 us (6%)
    pallas_call x1, Pallas kernels, on_device(): pl.pallas_call(whole_kernel, out_shape=(jax.ShapeDtypeStruct((2 * slots,...  41.8 us
    dot_general x1, matrix products, on_device(): jnp.einsum('scpr,cst->prt', mine, table, preferred_element_type=jnp.float32)  2.47 us

profile of v7, /device:TPU:1, one launch (start us, length us, event | category | flops | bytes accessed | tf_op | source)
XLA Modules:
  0.0 44.3 jit_solution(16850801174228562187)
XLA Ops:
  0.0 41.8 %whole.1 = (bf16[512,512]{1,0:T(8,128)(2,1)}, bf16[32,8,8,128]{3,2,1,0:T(8,128)(2,1)}) custom-call(bf16[4,128,512]{2,1,0:T(8,128)(2,1)} %images_ref.1, bf16[128,128,128]{2,1,0:T(8,128)(2,1)} %radial_ref.1, s32[128]{0:T(128)} %first_ref.1, s32[128]{0:T(128)} %count_ref.1, s32[2,128]{1,0:T(2,128)} %bitcast.13, f32[128,16,128]{2,1,0:T(8,128)} %start_ref.1), custom_call_target="tpu_custom_call" | custom-call | tf_op jit(solution)/shard_map/whole/pallas_call | solution.py:310
  41.8 2.5 %fusion = bf16[4,128,512]{2,1,0:T(8,128)(2,1)} fusion(bf16[2,256,512,1]{2,1,0,3:T(8,128)(2,1)} %bitcast.11, bf16[256,2,4,128]{3,2,1,0:T(4,128)(2,1)} %bitcast.12), kind=kOutput, calls=%fused_computation.1 | convolution fusion | flops 268697600 | bytes 1572864 | tf_op jit(solution)/shard_map/scpr,cst->prt/dot_general | solution.py:347

commit v8 on v7

--- a/solution.py
+++ b/solution.py
@@ -26,12 +26,35 @@
     )
 
 
+def split(value, pieces):
+    out = []
+    for _ in range(pieces):
+        piece = value.astype(jnp.bfloat16)
+        value = value - piece.astype(jnp.float32)
+        out.append(piece)
+    return out
+
+
+def times_cov(basis_t, cov_high, cov_low):
+    rank = basis_t.shape[0]
+    high, low = split(basis_t, 2)
+    both = jnp.dot(
+        jnp.concatenate([high, low], axis=0), cov_high, preferred_element_type=jnp.float32
+    )
+    rest = jnp.dot(high, cov_low, preferred_element_type=jnp.float32)
+    return both[:rank] + (both[rank:] + rest)
+
+
 def orthonormal(image_t):
     rank, width = image_t.shape
     gram = dot32(image_t, image_t, ((1,), (1,)))
     lane_block = lax.broadcasted_iota(jnp.int32, (rank, rank * width), 1) // width
     spread = lane_block == lax.broadcasted_iota(jnp.int32, (rank, rank * width), 0)
-    wide = dot32(gram, spread.astype(jnp.float32), ((1,), (0,)))
+    pieces = jnp.concatenate(split(gram, 3), axis=0)
+    wide = jnp.dot(
+        pieces, jnp.where(spread, 1.0, 0.0).astype(jnp.bfloat16), preferred_element_type=jnp.float32
+    )
+    wide = wide[:rank] + wide[rank : 2 * rank] + wide[2 * rank :]
     cols = [wide[:, j * width : (j + 1) * width] for j in range(rank)]
     row_id = lax.broadcasted_iota(jnp.int32, (rank, width), 0)
     pivots = jnp.ones((rank, width), jnp.float32)
@@ -236,7 +259,6 @@
     own.wait()
 
     peers = list(z_peers())
-    waiting = None
     for part, spots in enumerate(SLOT_PARTS):
         wait_part(part, spec_ref, rows_ref, send_1, recv_1)
         for i in spots:
@@ -249,22 +271,20 @@
                 coef, coef, (((0,), (0,)), ((), ())), preferred_element_type=jnp.float32
             )
             if i < len(peers):
+                _, there, pd = peers[i]
                 given_ref[i] = cov.astype(jnp.bfloat16)
+                remote(given_ref.at[i], taken_ref.at[there], send_2, recv_2, (pd, o)).start()
             else:
                 part_ref[...] = cov
-            if waiting is not None:
-                waiting.start()
-            if i < len(peers):
-                _, there, pd = peers[i]
-                waiting = remote(given_ref.at[i], taken_ref.at[there], send_2, recv_2, (pd, o))
     wait_blocks(given_ref, taken_ref, send_2, recv_2, NZ - 1)
     cov = part_ref[...]
     for i in range(NZ - 1):
         cov = cov + taken_ref[i].astype(jnp.float32)
 
+    cov_high, cov_low = split(cov, 2)
     basis_t = start_own[...]
     for step in range(ITERS):
-        basis_t = orthonormal(dot32(basis_t, cov, ((1,), (0,))))
+        basis_t = orthonormal(times_cov(basis_t, cov_high, cov_low))
     eig_t = basis_t.astype(jnp.bfloat16)
     eigs_ref[NZ - 1] = eig_t
     for i, there, pd in peers:

time: 44.4 us -> 43.7 us (0.984)
  Pallas kernels: 41.8 us -> 41.1 us
    pallas_call x1, Pallas kernels: 41.8 us -> 41.1 us  [on_device(): pl.pallas_call(whole_kernel, out_shape=(jax.ShapeDtypeStruct((2 * slots,...]
where the time goes in v8:
time: 43.7 us; the launch traced here: 43.6 us
  Pallas kernels  41.1 us (94%)
  matrix products  2.47 us (6%)
    pallas_call x1, Pallas kernels, on_device(): pl.pallas_call(whole_kernel, out_shape=(jax.ShapeDtypeStruct((2 * slots,...  41.1 us
    dot_general x1, matrix products, on_device(): jnp.einsum('scpr,cst->prt', mine, table, preferred_element_type=jnp.float32)  2.47 us

profile of v8, /device:TPU:1, one launch (start us, length us, event | category | flops | bytes accessed | tf_op | source)
XLA Modules:
  0.0 43.6 jit_solution(12639547791391067543)
XLA Ops:
  0.0 41.1 %whole.1 = (bf16[512,512]{1,0:T(8,128)(2,1)}, bf16[32,8,8,128]{3,2,1,0:T(8,128)(2,1)}) custom-call(bf16[4,128,512]{2,1,0:T(8,128)(2,1)} %images_ref.1, bf16[128,128,128]{2,1,0:T(8,128)(2,1)} %radial_ref.1, s32[128]{0:T(128)} %first_ref.1, s32[128]{0:T(128)} %count_ref.1, s32[2,128]{1,0:T(2,128)} %bitcast.13, f32[128,16,128]{2,1,0:T(8,128)} %start_ref.1), custom_call_target="tpu_custom_call" | custom-call | tf_op jit(solution)/shard_map/whole/pallas_call | solution.py:330
  41.1 2.5 %fusion = bf16[4,128,512]{2,1,0:T(8,128)(2,1)} fusion(bf16[2,256,512,1]{2,1,0,3:T(8,128)(2,1)} %bitcast.11, bf16[256,2,4,128]{3,2,1,0:T(4,128)(2,1)} %bitcast.12), kind=kOutput, calls=%fused_computation.1 | convolution fusion | flops 268697600 | bytes 1572864 | tf_op jit(solution)/shard_map/scpr,cst->prt/dot_general | solution.py:367

commit v9 on v8

--- a/solution.py
+++ b/solution.py
@@ -43,6 +43,23 @@
     )
     rest = jnp.dot(high, cov_low, preferred_element_type=jnp.float32)
     return both[:rank] + (both[rank:] + rest)
+
+
+def fold(cov):
+    lane = lax.broadcasted_iota(jnp.int32, (32, 128), 1)
+    second = jnp.where(lane < 32, pltpu.roll(cov[96:], 32, 1), cov[32:64])
+    third = jnp.where(lane[:16] < 64, pltpu.roll(cov[80:96], 64, 1), cov[64:80])
+    return jnp.concatenate([cov[:32], second, third], axis=0)
+
+
+def unfold(folded):
+    second, third = folded[32:64], folded[64:]
+    upper = jnp.concatenate(
+        [folded[:32], second, third, pltpu.roll(third, 64, 1), pltpu.roll(second, 96, 1)], axis=0
+    )
+    row_block = lax.broadcasted_iota(jnp.int32, (128, 128), 0) // 32
+    lane_block = lax.broadcasted_iota(jnp.int32, (128, 128), 1) // 32
+    return jnp.where(row_block > lane_block, upper.T, upper)
 
 
 def orthonormal(image_t):
@@ -267,8 +284,10 @@
                 rows.astype(jnp.bfloat16), masked_ref[i], preferred_element_type=jnp.float32
             ).astype(jnp.bfloat16)
             coef_ref[i] = coef
-            cov = lax.dot_general(
-                coef, coef, (((0,), (0,)), ((), ())), preferred_element_type=jnp.float32
+            cov = fold(
+                lax.dot_general(
+                    coef, coef, (((0,), (0,)), ((), ())), preferred_element_type=jnp.float32
+                )
             )
             if i < len(peers):
                 _, there, pd = peers[i]
@@ -281,7 +300,7 @@
     for i in range(NZ - 1):
         cov = cov + taken_ref[i].astype(jnp.float32)
 
-    cov_high, cov_low = split(cov, 2)
+    cov_high, cov_low = split(unfold(cov), 2)
     basis_t = start_own[...]
     for step in range(ITERS):
         basis_t = orthonormal(times_cov(basis_t, cov_high, cov_low))
@@ -342,9 +361,9 @@
             pltpu.VMEM((NZ, radial_rows, width), jnp.bfloat16),
             pltpu.VMEM((NZ, radial_rows, width), jnp.bfloat16),
             pltpu.VMEM((NZ, NPLANE * 2 * particles, width), jnp.bfloat16),
-            pltpu.VMEM((width, width), jnp.float32),
-            pltpu.VMEM((NZ, width, width), jnp.bfloat16),
-            pltpu.VMEM((NZ, width, width), jnp.bfloat16),
+            pltpu.VMEM((80, width), jnp.float32),
+            pltpu.VMEM((NZ, 80, width), jnp.bfloat16),
+            pltpu.VMEM((NZ, 80, width), jnp.bfloat16),
             pltpu.VMEM((NZ, rank, width), jnp.bfloat16),
             pltpu.VMEM(blocks, jnp.bfloat16),
             pltpu.VMEM((rank, width), jnp.float32),

time: 43.7 us -> 41.6 us (0.952)
  Pallas kernels: 41.1 us -> 39 us
    pallas_call x1, Pallas kernels: 41.1 us -> 39 us  [on_device(): pl.pallas_call(whole_kernel, out_shape=(jax.ShapeDtypeStruct((2 * slots,...]
where the time goes in v9:
time: 41.6 us; the launch traced here: 41.5 us
  Pallas kernels  39 us (94%)
  matrix products  2.47 us (6%)
    pallas_call x1, Pallas kernels, on_device(): pl.pallas_call(whole_kernel, out_shape=(jax.ShapeDtypeStruct((2 * slots,...  39 us
    dot_general x1, matrix products, on_device(): jnp.einsum('scpr,cst->prt', mine, table, preferred_element_type=jnp.float32)  2.47 us

profile of v9, /device:TPU:1, one launch (start us, length us, event | category | flops | bytes accessed | tf_op | source)
XLA Modules:
  0.0 41.5 jit_solution(3013286280957481149)
XLA Ops:
  0.0 39.0 %whole.1 = (bf16[512,512]{1,0:T(8,128)(2,1)}, bf16[32,8,8,128]{3,2,1,0:T(8,128)(2,1)}) custom-call(bf16[4,128,512]{2,1,0:T(8,128)(2,1)} %images_ref.1, bf16[128,128,128]{2,1,0:T(8,128)(2,1)} %radial_ref.1, s32[128]{0:T(128)} %first_ref.1, s32[128]{0:T(128)} %count_ref.1, s32[2,128]{1,0:T(2,128)} %bitcast.13, f32[128,16,128]{2,1,0:T(8,128)} %start_ref.1), custom_call_target="tpu_custom_call" | custom-call | tf_op jit(solution)/shard_map/whole/pallas_call | solution.py:349
  39.0 2.5 %fusion = bf16[4,128,512]{2,1,0:T(8,128)(2,1)} fusion(bf16[2,256,512,1]{2,1,0,3:T(8,128)(2,1)} %bitcast.11, bf16[256,2,4,128]{3,2,1,0:T(4,128)(2,1)} %bitcast.12), kind=kOutput, calls=%fused_computation.1 | convolution fusion | flops 268697600 | bytes 1572864 | tf_op jit(solution)/shard_map/scpr,cst->prt/dot_general | solution.py:386

commit v10 on v9

--- a/solution.py
+++ b/solution.py
@@ -216,8 +216,10 @@
     count_ref,
     order_ref,
     start_ref,
+    table_out,
+    out_ref,
     table_ref,
-    out_ref,
+    back_ref,
     wide_ref,
     spec_ref,
     rows_ref,
@@ -242,6 +244,7 @@
     own_4,
     load_1,
     load_2,
+    store_1,
 ):
     d, o, z, y, x = place()
     first_slot = (y * NX + x) * NZ
@@ -255,6 +258,8 @@
     radial_load.start()
     start_load.start()
     fill_table(order_ref, table_ref)
+    table_store = pltpu.make_async_copy(table_ref, table_out, store_1)
+    table_store.start()
     fill_spectrum(table_ref, images_ref, wide_ref)
     spec_ref[...] = wide_ref[...].reshape(spec_ref.shape).astype(jnp.bfloat16)
     radial_load.wait()
@@ -326,16 +331,26 @@
             ).astype(jnp.bfloat16)
             profile = jnp.dot(scores, u_t, preferred_element_type=jnp.float32)
             prof_ref[:, i] = profile.reshape(NPLANE, 8, radial_rows).astype(jnp.bfloat16)
-        send_part(part, prof_ref, out_ref, send_4, recv_4)
-    own = own_block(prof_ref, out_ref, own_4)
+        send_part(part, prof_ref, back_ref, send_4, recv_4)
+    own = own_block(prof_ref, back_ref, own_4)
     own.start()
     for i, _, pd in peers:
         remote(
             eigs_ref.at[NZ - 1], eigs_ref.at[i], send_3.at[i], recv_3.at[i], (pd, o)
         ).wait_send()
     own.wait()
+
+    by_slot = wide_ref.reshape(*back_ref.shape)
     for part in reversed(range(len(SLOT_PARTS))):
-        wait_part(part, prof_ref, out_ref, send_4, recv_4)
+        wait_part(part, prof_ref, back_ref, send_4, recv_4)
+        for i in SLOT_PARTS[part]:
+            by_slot[:, i] = back_ref[:, i].astype(jnp.float32)
+    slots = NPLANE * NZ
+    for p in range(out_ref.shape[0]):
+        for c in range(2):
+            ordered = wide_ref[pl.ds(4 * c + p, slots, stride=8), :]
+            out_ref[p, slots * c : slots * (c + 1), :] = ordered.astype(jnp.bfloat16)
+    table_store.wait()
 
 
 def on_device(polar_images, radial_basis, radial_start, radial_count, order_of_slot, start_block):
@@ -350,11 +365,13 @@
         whole_kernel,
         out_shape=(
             jax.ShapeDtypeStruct((2 * slots, angles), jnp.bfloat16),
-            jax.ShapeDtypeStruct(blocks, jnp.bfloat16),
+            jax.ShapeDtypeStruct((particles, 2 * slots, radial_rows), jnp.bfloat16),
         ),
         in_specs=[vmem, anywhere, smem, smem, vmem, anywhere],
-        out_specs=(vmem, vmem),
+        out_specs=(anywhere, vmem),
         scratch_shapes=[
+            pltpu.VMEM((2 * slots, angles), jnp.bfloat16),
+            pltpu.VMEM(blocks, jnp.bfloat16),
             pltpu.VMEM((slots * 2 * particles, radial_rows), jnp.float32),
             pltpu.VMEM(blocks, jnp.bfloat16),
             pltpu.VMEM(blocks, jnp.bfloat16),
@@ -369,7 +386,7 @@
             pltpu.VMEM((rank, width), jnp.float32),
             *[pltpu.SemaphoreType.DMA((len(SLOT_PARTS),))] * 4,
             *[pltpu.SemaphoreType.DMA((NZ - 1,))] * 2,
-            *[pltpu.SemaphoreType.DMA] * 6,
+            *[pltpu.SemaphoreType.DMA] * 7,
         ],
         compiler_params=pltpu.CompilerParams(collective_id=0, has_side_effects=True),
         name="whole",
@@ -381,9 +398,7 @@
         order_of_slot.reshape(2, slots // 2),
         start_block,
     )
-    mine = mine.reshape(slots, 2, particles, radial_rows)
-    table = table.reshape(2, slots, angles)
-    denoised = jnp.einsum("scpr,cst->prt", mine, table, preferred_element_type=jnp.float32)
+    denoised = jnp.einsum("per,et->prt", mine, table, preferred_element_type=jnp.float32)
     return denoised.astype(jnp.bfloat16)
 
 

time: 41.6 us -> 41.6 us (level)
  no operation moved by 1% of the time
where the time goes in v10:
time: 41.6 us; the launch traced here: 41.5 us
  Pallas kernels  39 us (94%)
  matrix products  2.46 us (6%)
    pallas_call x1, Pallas kernels, on_device(): pl.pallas_call(whole_kernel, out_shape=(jax.ShapeDtypeStruct((2 * slots,...  39 us
    dot_general x1, matrix products, on_device(): jnp.einsum('per,et->prt', mine, table, preferred_element_type=jnp.float32)  2.46 us

profile of v10, /device:TPU:1, one launch (start us, length us, event | category | flops | bytes accessed | tf_op | source)
XLA Modules:
  0.0 41.5 jit_solution(16951100994258825319)
XLA Ops:
  0.0 39.0 %whole.1 = (bf16[512,512]{1,0:T(8,128)(2,1)}, bf16[4,512,128]{2,1,0:T(8,128)(2,1)}) custom-call(bf16[4,128,512]{2,1,0:T(8,128)(2,1)} %images_ref.1, bf16[128,128,128]{2,1,0:T(8,128)(2,1)} %radial_ref.1, s32[128]{0:T(128)} %first_ref.1, s32[128]{0:T(128)} %count_ref.1, s32[2,128]{1,0:T(2,128)} %bitcast.5, f32[128,16,128]{2,1,0:T(8,128)} %start_ref.1), custom_call_target="tpu_custom_call" | custom-call | tf_op jit(solution)/shard_map/whole/pallas_call | solution.py:364
  39.0 2.5 %convolution_convert_fusion = bf16[4,128,512]{2,1,0:T(8,128)(2,1)} fusion(bf16[4,512,128]{2,1,0:T(8,128)(2,1)} %get-tuple-element.7, bf16[512,512]{1,0:T(8,128)(2,1)} %get-tuple-element.8), kind=kOutput, calls=%fused_computation | convolution fusion | flops 268697600 | bytes 1572864 | tf_op jit(solution)/shard_map/per,et->prt/dot_general | solution.py:401

commit v11 on v10

--- a/solution.py
+++ b/solution.py
@@ -210,14 +210,18 @@
 
 
 def whole_kernel(
+    images_in,
+    radial_ref,
+    first_in,
+    count_in,
+    order_in,
+    start_ref,
+    table_out,
+    out_ref,
     images_ref,
-    radial_ref,
     first_ref,
     count_ref,
     order_ref,
-    start_ref,
-    table_out,
-    out_ref,
     table_ref,
     back_ref,
     wide_ref,
@@ -245,6 +249,10 @@
     load_1,
     load_2,
     store_1,
+    load_3,
+    load_4,
+    load_5,
+    load_6,
 ):
     d, o, z, y, x = place()
     first_slot = (y * NX + x) * NZ
@@ -253,17 +261,29 @@
         pl.semaphore_signal(barrier, inc=1, device_id=(pd, o), device_id_type=MESH)
     for _, pd, po in plane_peers():
         pl.semaphore_signal(barrier, inc=1, device_id=(pd, po), device_id_type=MESH)
+    order_load = pltpu.make_async_copy(order_in, order_ref, load_3)
+    images_load = pltpu.make_async_copy(images_in, images_ref, load_4)
+    first_load = pltpu.make_async_copy(first_in, first_ref, load_5)
+    count_load = pltpu.make_async_copy(count_in, count_ref, load_6)
+    order_load.start()
+    images_load.start()
+    first_load.start()
+    count_load.start()
     radial_load = pltpu.make_async_copy(radial_ref.at[pl.ds(first_slot, NZ)], radial_own, load_1)
     start_load = pltpu.make_async_copy(start_ref.at[first_slot + z], start_own, load_2)
     radial_load.start()
     start_load.start()
+    order_load.wait()
     fill_table(order_ref, table_ref)
     table_store = pltpu.make_async_copy(table_ref, table_out, store_1)
     table_store.start()
+    images_load.wait()
     fill_spectrum(table_ref, images_ref, wide_ref)
     spec_ref[...] = wide_ref[...].reshape(spec_ref.shape).astype(jnp.bfloat16)
     radial_load.wait()
     start_load.wait()
+    first_load.wait()
+    count_load.wait()
     radial_rows, width = masked_ref.shape[1:]
     row_id = lax.broadcasted_iota(jnp.int32, (radial_rows, width), 0)
     col_id = lax.broadcasted_iota(jnp.int32, (radial_rows, width), 1)
@@ -359,7 +379,6 @@
     slots = order_of_slot.shape[0]
     blocks = (NPLANE, NZ, 2 * particles, radial_rows)
     vmem = pl.BlockSpec(memory_space=pltpu.VMEM)
-    smem = pl.BlockSpec(memory_space=pltpu.SMEM)
     anywhere = pl.BlockSpec(memory_space=pl.ANY)
     table, mine = pl.pallas_call(
         whole_kernel,
@@ -367,9 +386,13 @@
             jax.ShapeDtypeStruct((2 * slots, angles), jnp.bfloat16),
             jax.ShapeDtypeStruct((particles, 2 * slots, radial_rows), jnp.bfloat16),
         ),
-        in_specs=[vmem, anywhere, smem, smem, vmem, anywhere],
+        in_specs=[anywhere] * 6,
         out_specs=(anywhere, vmem),
         scratch_shapes=[
+            pltpu.VMEM(polar_images.shape, jnp.bfloat16),
+            pltpu.SMEM(radial_start.shape, jnp.int32),
+            pltpu.SMEM(radial_count.shape, jnp.int32),
+            pltpu.VMEM((2, slots // 2), jnp.int32),
             pltpu.VMEM((2 * slots, angles), jnp.bfloat16),
             pltpu.VMEM(blocks, jnp.bfloat16),
             pltpu.VMEM((slots * 2 * particles, radial_rows), jnp.float32),
@@ -386,7 +409,7 @@
             pltpu.VMEM((rank, width), jnp.float32),
             *[pltpu.SemaphoreType.DMA((len(SLOT_PARTS),))] * 4,
             *[pltpu.SemaphoreType.DMA((NZ - 1,))] * 2,
-            *[pltpu.SemaphoreType.DMA] * 7,
+            *[pltpu.SemaphoreType.DMA] * 11,
         ],
         compiler_params=pltpu.CompilerParams(collective_id=0, has_side_effects=True),
         name="whole",

time: 41.6 us -> 40.5 us (0.974)
  Pallas kernels: 39 us -> 37.9 us
    pallas_call x1, Pallas kernels: 39 us -> 37.9 us  [on_device(): pl.pallas_call(whole_kernel, out_shape=(jax.ShapeDtypeStruct((2 * slots,...]
where the time goes in v11:
time: 40.5 us; the launch traced here: 40.4 us
  Pallas kernels  37.9 us (94%)
  matrix products  2.46 us (6%)
    pallas_call x1, Pallas kernels, on_device(): pl.pallas_call(whole_kernel, out_shape=(jax.ShapeDtypeStruct((2 * slots,...  37.9 us
    dot_general x1, matrix products, on_device(): jnp.einsum('per,et->prt', mine, table, preferred_element_type=jnp.float32)  2.46 us

profile of v11, /device:TPU:1, one launch (start us, length us, event | category | flops | bytes accessed | tf_op | source)
XLA Modules:
  0.0 40.4 jit_solution(2968391771179087772)
XLA Ops:
  0.0 37.9 %whole.1 = (bf16[512,512]{1,0:T(8,128)(2,1)}, bf16[4,512,128]{2,1,0:T(8,128)(2,1)}) custom-call(bf16[4,128,512]{2,1,0:T(8,128)(2,1)} %images_in.1, bf16[128,128,128]{2,1,0:T(8,128)(2,1)} %radial_ref.1, s32[128]{0:T(128)} %first_in.1, s32[128]{0:T(128)} %count_in.1, s32[2,128]{1,0:T(2,128)} %bitcast.5, f32[128,16,128]{2,1,0:T(8,128)} %start_ref.1), custom_call_target="tpu_custom_call" | custom-call | tf_op jit(solution)/shard_map/whole/pallas_call | solution.py:383
  37.9 2.5 %convolution_convert_fusion = bf16[4,128,512]{2,1,0:T(8,128)(2,1)} fusion(bf16[4,512,128]{2,1,0:T(8,128)(2,1)} %get-tuple-element.7, bf16[512,512]{1,0:T(8,128)(2,1)} %get-tuple-element.8), kind=kOutput, calls=%fused_computation | convolution fusion | flops 268697600 | bytes 1572864 | tf_op jit(solution)/shard_map/per,et->prt/dot_general | solution.py:424

commit v12 on v11

--- a/solution.py
+++ b/solution.py
@@ -217,6 +217,7 @@
     order_in,
     start_ref,
     table_out,
+    profile_out,
     out_ref,
     images_ref,
     first_ref,
@@ -253,6 +254,7 @@
     load_4,
     load_5,
     load_6,
+    store_2,
 ):
     d, o, z, y, x = place()
     first_slot = (y * NX + x) * NZ
@@ -366,10 +368,15 @@
         for i in SLOT_PARTS[part]:
             by_slot[:, i] = back_ref[:, i].astype(jnp.float32)
     slots = NPLANE * NZ
+    stores = []
     for p in range(out_ref.shape[0]):
         for c in range(2):
             ordered = wide_ref[pl.ds(4 * c + p, slots, stride=8), :]
             out_ref[p, slots * c : slots * (c + 1), :] = ordered.astype(jnp.bfloat16)
+        stores.append(pltpu.make_async_copy(out_ref.at[p], profile_out.at[p], store_2.at[p]))
+        stores[-1].start()
+    for store in stores:
+        store.wait()
     table_store.wait()
 
 
@@ -378,7 +385,6 @@
     rank, width = start_block.shape[1:]
     slots = order_of_slot.shape[0]
     blocks = (NPLANE, NZ, 2 * particles, radial_rows)
-    vmem = pl.BlockSpec(memory_space=pltpu.VMEM)
     anywhere = pl.BlockSpec(memory_space=pl.ANY)
     table, mine = pl.pallas_call(
         whole_kernel,
@@ -387,8 +393,9 @@
             jax.ShapeDtypeStruct((particles, 2 * slots, radial_rows), jnp.bfloat16),
         ),
         in_specs=[anywhere] * 6,
-        out_specs=(anywhere, vmem),
+        out_specs=(anywhere, anywhere),
         scratch_shapes=[
+            pltpu.VMEM((particles, 2 * slots, radial_rows), jnp.bfloat16),
             pltpu.VMEM(polar_images.shape, jnp.bfloat16),
             pltpu.SMEM(radial_start.shape, jnp.int32),
             pltpu.SMEM(radial_count.shape, jnp.int32),
@@ -410,6 +417,7 @@
             *[pltpu.SemaphoreType.DMA((len(SLOT_PARTS),))] * 4,
             *[pltpu.SemaphoreType.DMA((NZ - 1,))] * 2,
             *[pltpu.SemaphoreType.DMA] * 11,
+            pltpu.SemaphoreType.DMA((particles,)),
         ],
         compiler_params=pltpu.CompilerParams(collective_id=0, has_side_effects=True),
         name="whole",

time: 40.5 us -> 40.4 us (level)
  no operation moved by 1% of the time
where the time goes in v12:
time: 40.4 us; the launch traced here: 40.3 us
  Pallas kernels  37.8 us (94%)
  matrix products  2.46 us (6%)
    pallas_call x1, Pallas kernels, on_device(): pl.pallas_call(whole_kernel, out_shape=(jax.ShapeDtypeStruct((2 * slots,...  37.8 us
    dot_general x1, matrix products, on_device(): jnp.einsum('per,et->prt', mine, table, preferred_element_type=jnp.float32)  2.46 us

profile of v12, /device:TPU:1, one launch (start us, length us, event | category | flops | bytes accessed | tf_op | source)
XLA Modules:
  0.0 40.3 jit_solution(16723075271045508425)
XLA Ops:
  0.0 37.8 %whole.1 = (bf16[512,512]{1,0:T(8,128)(2,1)}, bf16[4,512,128]{2,1,0:T(8,128)(2,1)}) custom-call(bf16[4,128,512]{2,1,0:T(8,128)(2,1)} %images_in.1, bf16[128,128,128]{2,1,0:T(8,128)(2,1)} %radial_ref.1, s32[128]{0:T(128)} %first_in.1, s32[128]{0:T(128)} %count_in.1, s32[2,128]{1,0:T(2,128)} %bitcast.5, f32[128,16,128]{2,1,0:T(8,128)} %start_ref.1), custom_call_target="tpu_custom_call" | custom-call | tf_op jit(solution)/shard_map/whole/pallas_call | solution.py:389
  37.8 2.5 %convolution_convert_fusion = bf16[4,128,512]{2,1,0:T(8,128)(2,1)} fusion(bf16[4,512,128]{2,1,0:T(8,128)(2,1)} %get-tuple-element.7, bf16[512,512]{1,0:T(8,128)(2,1)} %get-tuple-element.8), kind=kOutput, calls=%fused_computation | convolution fusion | flops 268697600 | bytes 1572864 | tf_op jit(solution)/shard_map/per,et->prt/dot_general | solution.py:432
